TPU v7x, 256 devices: a whole 4x4x8 slice. The times are simulated.
256 devices in a mesh: ctx: 32 (over x, z_hi, y), exp: 8 (over z_lo, core).
Axes of the slice: x: 4, y: 4, z: 8 (z_hi: 2, z_lo: 4; z = z_hi * 4 + z_lo), core: 2. Of those that a mesh axis runs over, the one named last changes fastest.
Arguments:
- queries: bfloat16 [256, 32, 128], P(None, 'exp'), may hold values from -64 to 64
- keys: bfloat16 [32768, 8, 128], P('ctx', 'exp'), may hold values from -8 to 8
- values: bfloat16 [32768, 8, 128], P('ctx', 'exp'), may hold values from -32 to 32
- out_proj: bfloat16 [4096, 4096], P('exp', 'ctx'), may hold values from -0.09375 to 0.09375
- residual: bfloat16 [256, 4096], P('ctx'), may hold values from -6 to 6
- gain: float32 [4096], replicated, may hold values from 0.1 to 1.9
- routes: int32 [256, 2], P('ctx'), may hold values from 0 to 7, all different within a row; in each aligned block of 8 rows (0 to 7, 8 to 15, ...) at most 4 rows name the same one
- gates: float32 [256, 2], P('ctx'), may hold values from 0.25 to 1
- w_gate: bfloat16 [8, 4096, 14336], P('exp', None, 'ctx'), may hold values from -0.09375 to 0.09375
- w_up: bfloat16 [8, 4096, 14336], P('exp', None, 'ctx'), may hold values from -0.09375 to 0.09375
- w_down: bfloat16 [8, 14336, 4096], P('exp', 'ctx'), may hold values from -0.046875 to 0.046875
Outputs:
- mixed: bfloat16 [256, 4096], P('ctx', 'exp')
Inputs may be any that keep to these rules, and one draw needn't show every extreme that they name: `routes`: within each aligned block of 8 rows no expert is named by more than 4 rows, some expert is named by exactly 4 rows in some block, and the 2 experts of a row differ.
All inputs are finite; a program needn't handle non-finite values.
Results may differ from a plain program's by a relative error of at most 0.017.
Values may be sent and summed in bfloat16 or wider, within the bound.
A program may use at most 128 MiB of HBM per device.

v0:
```python
import math

import jax
import jax.numpy as jnp
from jax import lax
from jax.sharding import PartitionSpec as P


def joined(part, axis, combine):
    gathered = jax.tree.map(lambda a: lax.all_gather(a, axis), part)

    def take(source):
        return jax.tree.map(lambda a: lax.dynamic_index_in_dim(a, source, 0, False), gathered)

    return lax.fori_loop(
        1, lax.axis_size(axis), lambda source, state: combine(state, take(source)), take(0)
    )


def combine_parts(first_part, second_part):
    top_level = jnp.maximum(first_part[0], second_part[0])
    first_scale = jnp.exp(first_part[0] - top_level)
    second_scale = jnp.exp(second_part[0] - top_level)
    summed = first_part[1] * first_scale + second_part[1] * second_scale
    weighted = first_part[2] * first_scale[..., None] + second_part[2] * second_scale[..., None]
    return (top_level, summed, weighted)


def local(queries, keys, values, out_proj, residual, gain, routes, gates, w_gate, w_up, w_down):
    tokens_all, heads_local, head_dim = queries.shape
    key_rows, kv_local, unused_dim = keys.shape
    groups = heads_local // kv_local
    ctx_count = lax.axis_size("ctx")
    ctx_index = lax.axis_index("ctx")
    exp_index = lax.axis_index("exp")
    block_rows = residual.shape[0]
    total_len = key_rows * ctx_count
    score_scale = 1.0 / math.sqrt(head_dim)
    grouped = queries.reshape(tokens_all, kv_local, groups, head_dim)
    scores = (
        jnp.einsum("tgrd,sgd->gtrs", grouped, keys, preferred_element_type=jnp.float32)
        * score_scale
    )
    key_pos = ctx_index * key_rows + jnp.arange(key_rows, dtype=jnp.int32)
    query_pos = total_len - tokens_all + jnp.arange(tokens_all, dtype=jnp.int32)
    visible = (key_pos[None, :] <= query_pos[:, None])[None, :, None, :]
    scores = jnp.where(visible, scores, jnp.float32(-1e30))
    block_max = jnp.max(scores, axis=-1)
    expw = jnp.where(visible, jnp.exp(scores - block_max[..., None]), jnp.float32(0.0))
    block_sum = jnp.sum(expw, axis=-1)
    block_out = jnp.einsum(
        "gtrs,sgd->gtrd", expw.astype(jnp.bfloat16), values, preferred_element_type=jnp.float32
    )
    merged = joined((block_max, block_sum, block_out), "ctx", combine_parts)
    attended_all = merged[2] / merged[1][..., None]
    own_rows = lax.dynamic_slice_in_dim(attended_all, ctx_index * block_rows, block_rows, 1)
    attended = (
        own_rows.transpose(1, 0, 2, 3)
        .reshape(block_rows, heads_local * head_dim)
        .astype(jnp.bfloat16)
    )
    partial_value = jnp.dot(
        attended,
        lax.all_gather(out_proj, "ctx", axis=1, tiled=True),
        preferred_element_type=jnp.float32,
    )
    stream = residual.astype(jnp.float32) + lax.psum(
        partial_value.astype(jnp.bfloat16), "exp"
    ).astype(jnp.float32)
    normed = (
        stream * lax.rsqrt(jnp.mean(stream * stream, axis=-1, keepdims=True) + 1e-05) * gain
    ).astype(jnp.bfloat16)
    experts_local = w_gate.shape[0]
    expert_count = experts_local * lax.axis_size("exp")
    top_count = routes.shape[1]
    capacity = min(block_rows, 2 * top_count * block_rows // expert_count)
    flat_ids = routes.reshape(block_rows * top_count)
    onehot = (flat_ids[:, None] == jnp.arange(expert_count, dtype=jnp.int32)[None, :]).astype(
        jnp.int32
    )
    before = jnp.cumsum(onehot, axis=0, dtype=jnp.int32) - onehot
    slot_of = jnp.sum(before * onehot, axis=1, dtype=jnp.int32)
    mine_ids = exp_index * experts_local + jnp.arange(experts_local, dtype=jnp.int32)
    is_mine = flat_ids[:, None] == mine_ids[None, :]
    slot_hit = is_mine[:, :, None] & (
        slot_of[:, None, None] == jnp.arange(capacity, dtype=jnp.int32)[None, None, :]
    )
    slot_hit = slot_hit.astype(jnp.float32).reshape(block_rows, top_count, experts_local, capacity)
    dispatch_map = jnp.sum(slot_hit, axis=1)
    combine_map = jnp.sum(slot_hit * gates[:, :, None, None], axis=1)
    buffer = jnp.einsum(
        "tec,td->ced", dispatch_map.astype(jnp.bfloat16), normed, preferred_element_type=jnp.float32
    ).astype(jnp.bfloat16)
    shard_rows = lax.all_gather(buffer, "ctx", axis=0, tiled=True)
    gate_val = jnp.einsum("ned,edf->nef", shard_rows, w_gate, preferred_element_type=jnp.float32)
    up_val = jnp.einsum("ned,edf->nef", shard_rows, w_up, preferred_element_type=jnp.float32)
    act = (jax.nn.silu(gate_val) * up_val).astype(jnp.bfloat16)
    expert_out = lax.psum_scatter(
        jnp.einsum("nef,efd->ned", act, w_down, preferred_element_type=jnp.float32).astype(
            jnp.bfloat16
        ),
        "ctx",
        scatter_dimension=0,
        tiled=True,
    ).astype(jnp.float32)
    contribution = jnp.einsum(
        "tec,ced->td", combine_map, expert_out, precision=lax.Precision.HIGHEST
    )
    moe_share = lax.psum_scatter(
        contribution.astype(jnp.bfloat16), "exp", scatter_dimension=1, tiled=True
    ).astype(jnp.float32)
    feat_width = moe_share.shape[1]
    own_stream = lax.dynamic_slice_in_dim(stream, exp_index * feat_width, feat_width, 1)
    return (own_stream + moe_share).astype(jnp.bfloat16)


def solution(mesh):
    return jax.shard_map(
        local,
        mesh=mesh,
        in_specs=(
            P(None, "exp", None),
            P("ctx", "exp", None),
            P("ctx", "exp", None),
            P("exp", "ctx"),
            P("ctx", None),
            P(),
            P("ctx", None),
            P("ctx", None),
            P("exp", None, "ctx"),
            P("exp", None, "ctx"),
            P("exp", "ctx", None),
        ),
        out_specs=P("ctx", "exp"),
        check_vma=False,
    )
```

profile of v0, /device:TPU:1, one launch (start us, length us, event | category | flops | bytes accessed | tf_op | source)
XLA Modules:
  0.0 1040.2 jit_solution(11815722336202214809)
XLA Ops:
  7.5 2.0 fusion.8
  9.5 2.0 copy-done.1
  11.4 2.2 fusion.16
  14.5 3.7 fusion.15
  18.1 109.1 %all-gather = f32[8192,4]{0,1:T(4,128)S(1)} all-gather(f32[256,4]{0,1:T(4,128)S(1)} %get-tuple-element.241), channel_id=2, replica_groups=mesh['ctx'=32,'exp'=8] {'ctx'}, dimensions={0}, use_global_device_ids=true | all-gather | bytes 135168 | tf_op jit(solution)/shard_map/all_gather | solution.py:10
  127.2 107.4 %all-gather.1 = f32[8192,4]{0,1:T(4,128)S(1)} all-gather(f32[256,4]{0,1:T(4,128)S(1)} %fusion.15), channel_id=3, replica_groups=mesh['ctx'=32,'exp'=8] {'ctx'}, dimensions={0}, use_global_device_ids=true | all-gather | bytes 135168 | tf_op jit(solution)/shard_map/all_gather | solution.py:10
  235.2 33.1 %all-gather.11.cloned.1.call-done = f32[8192,4,128]{2,0,1:T(8,128)} async-done(((f32[256,4,128]{2,0,1:T(8,128)}), f32[8192,4,128]{2,0,1:T(8,128)}) %all-gather.11.cloned.1.call-update) | async-done | bytes 16777232 | tf_op jit(solution)/shard_map/all_gather | solution.py:10
  269.8 84.7 %while.19 = (s32[]{:T(128)}, f32[1,256,4]{1,2,0:T(4,128)S(1)}, f32[1,256,4]{1,2,0:T(4,128)S(1)}, f32[1,256,4,128]{3,2,1,0:T(4,128)S(1)}, f32[32,1,256,4]{2,3,1,0...) while((s32[]{:T(128)}, f32[1,256,4]{1,2,0:T(4,128)S(1)}, ...), condition=%wide.region_3.4_spmd, body=%wide.region_2.3_spmd.sunk | while | flops 400389 | bytes 2699419 | solution.py:15
  271.2 1.3 fusion.75
  273.9 1.3 fusion.75
  282.2 1.3 fusion.75
  284.9 1.3 fusion.75
  287.6 1.3 fusion.75
  293.1 1.3 fusion.75
  295.8 1.3 fusion.75
  301.3 1.3 fusion.75
  309.5 1.3 fusion.75
  315.0 1.3 fusion.75
  323.2 1.3 fusion.75
  331.3 1.3 fusion.75
  339.6 1.3 fusion.75
  347.8 1.3 fusion.75
  354.8 44.8 %all-gather.7.cloned.1.call-done = bf16[512,4096]{1,0:T(8,128)(2,1)} async-done(((bf16[512,128]{1,0:T(8,128)(2,1)}), bf16[512,4096]{1,0:T(8,128)(2,1)}) %all-gather.7.cloned.1.call-update) | async-done | bytes 4194320 | tf_op jit(solution)/shard_map/all_gather | solution.py:64
  399.6 3.5 convolution_convert_fusion.2
  403.1 63.3 %all-reduce.4.cloned.1.call-done = bf16[8,4096]{1,0:T(8,128)(2,1)} async-done(((bf16[8,4096]{1,0:T(8,128)(2,1)}), bf16[8,4096]{1,0:T(8,128)(2,1)}) %all-reduce.4.cloned.1.call-update) | async-done | bytes 65552 | tf_op jit(solution)/shard_map/psum | solution.py:67
  469.2 92.7 %all-gather.9.cloned.1.call-done = bf16[128,1,4096]{2,1,0:T(2,128)(2,1)} async-done(((bf16[4,1,4096]{2,1,0:T(2,128)(2,1)}), bf16[128,1,4096]{2,1,0:T(2,128)(2,1)}) %all-gather.9.cloned.1.call-update) | async-done | bytes 1048592 | tf_op jit(solution)/shard_map/all_gather | solution.py:94
  561.9 4.8 fusion.19
  566.7 7.3 fusion.6
  575.3 400.3 %all-reduce.6.cloned.1.call-done = bf16[128,1,4096]{2,0,1:T(8,128)(2,1)} async-done(((bf16[128,1,4096]{2,0,1:T(8,128)(2,1)}), bf16[128,1,4096]{2,0,1:T(8,128)(2,1)}) %all-reduce.6.cloned.1.call-update) | async-done | bytes 1048592
  975.6 1.7 convolution_convert_fusion.1
  977.4 54.6 %reduce-scatter.3.cloned.1.call-done = bf16[8,512]{1,0:T(8,128)(2,1)} async-done(((bf16[8,4096]{1,0:T(8,128)(2,1)}), bf16[8,512]{1,0:T(8,128)(2,1)}) %reduce-scatter.3.cloned.1.call-update) | async-done | bytes 8208 | tf_op jit(solution)/shard_map/reduce_scatter | solution.py:109
  1032.0 1.3 add_convert_fusion
  (256 shorter events, 72.6 us)
Async XLA Ops:
  6.5 1.0 copy-start
  6.5 4.9 copy-start.7
  6.5 261.8 %all-gather.11.cloned.1.call-start = ((), (), s32[]{:S(2)}) async-start(), calls=%async_computation.5 | async-start | bytes 17301504 | tf_op jit(solution)/shard_map/all_gather | solution.py:10
  9.4 2.0 copy-start.1
  13.6 221.0 %copy-start.5 = (s32[8,2]{0,1:T(2,128)S(1)}, s32[8,2]{0,1:T(2,128)}, u32[]{:S(2)}) copy-start(s32[8,2]{0,1:T(2,128)} %param.19) | copy-start | bytes 196
  13.7 385.9 %all-gather.7.cloned.1.call-start = ((), (), s32[]{:S(2)}) async-start(), calls=%async_computation.1 | async-start | bytes 4325376 | tf_op jit(solution)/shard_map/all_gather | solution.py:64
  14.4 452.0 %all-reduce.4.cloned.1.call-start = ((), (), s32[]{:S(2)}) async-start(), calls=%async_computation.2 | async-start | bytes 131072 | tf_op jit(solution)/shard_map/psum | solution.py:67
  354.5 48.6 %copy-start.6 = (f32[8,2]{0,1:T(2,128)S(1)}, f32[8,2]{0,1:T(2,128)}, u32[]{:S(2)}) copy-start(f32[8,2]{0,1:T(2,128)} %param.20) | copy-start | bytes 196
  354.5 111.9 %copy-start.3 = (bf16[8,4096]{1,0:T(8,128)(2,1)S(1)}, bf16[8,4096]{1,0:T(8,128)(2,1)}, u32[]{:S(2)}) copy-start(bf16[8,4096]{1,0:T(8,128)(2,1)} %param.17) | copy-start | bytes 196612
  354.5 112.9 %copy-start.4 = (f32[4096]{0:T(1024)S(1)}, f32[4096]{0:T(1024)}, u32[]{:S(2)}) copy-start(f32[4096]{0:T(1024)} %param.18) | copy-start | bytes 49156
  403.1 158.9 %all-gather.9.cloned.1.call-start = ((), (), s32[]{:S(2)}) async-start(), calls=%async_computation.3 | async-start | bytes 2162688 | tf_op jit(solution)/shard_map/all_gather | solution.py:94
  469.2 506.4 %all-reduce.6.cloned.1.call-start = ((), (), s32[]{:S(2)}) async-start(), calls=%async_computation.6 | async-start | bytes 2097152
  561.9 4.8 copy-start.2
  566.7 7.4 copy-start.8
  574.0 458.0 %reduce-scatter.3.cloned.1.call-start = ((), (), s32[]{:S(2)}) async-start(), calls=%async_computation.4 | async-start | bytes 73728 | tf_op jit(solution)/shard_map/reduce_scatter | solution.py:109
Sparse Core Ops, SparseCore 0:
  13.8 254.5 all-gather.10
  271.5 127.9 all-gather.6
  403.2 63.2 all-reduce.3
  470.4 91.5 all-gather.8
  574.1 401.4 all-reduce.5
  978.0 53.9 reduce-scatter.2
where the time goes:
time: 1040 us
  waiting for transfers between devices  690 us (66%)
  blocking collectives  216 us (21%)
  local copies, waits for them, and re-layouts  48.1 us (5%)
  other arithmetic  47.1 us (5%)
  matrix products  22.4 us (2%)
  between operations  14.3 us (1%)
    unnamed x7, waiting for transfers between devices  401 us
    all_gather x2, blocking collectives, joined(): gathered = jax.tree.map(lambda a: lax.all_gather(a, axis), part)  216 us
    all_gather x1, waiting for transfers between devices, local(): shard_rows = lax.all_gather(buffer, 'ctx', axis=0, tiled=True)  92.7 us
    psum x1, waiting for transfers between devices, local(): lax.psum(partial_value.astype(jnp.bfloat16), 'exp').astype(jnp.float32)  63.3 us
    reduce_scatter x1, waiting for transfers between devices, local(): lax.psum_scatter(contribution.astype(jnp.bfloat16), 'exp', scatter_dimens...  54.6 us
    all_gather x1, waiting for transfers between devices, local(): lax.all_gather(out_proj, 'ctx', axis=1, tiled=True)  44.8 us
    add x31, other arithmetic, combine_parts(): first_part[2] * first_scale[..., None]  39.3 us
    dynamic_slice x31, local copies, waits for them, and re-layouts, take(): lax.dynamic_index_in_dim(a, source, 0, False)  33.8 us
  transfers between devices with their start and end apart: 6, of which 6 were waited for; matrix products, arithmetic and copies ran while one was open for 9% of the time, Pallas kernels for 0%

commit v1 on v0

v1 whole, which is shorter than its diff:
```python
import functools
import math

import jax
import jax.numpy as jnp
from jax import lax
from jax.experimental import pallas as pl
from jax.experimental.pallas import tpu as pltpu
from jax.sharding import PartitionSpec as P

F32 = jnp.float32
BF16 = jnp.bfloat16
PLANE = (4, 4)
CAP = 4
VMEM_LIMIT = 56 * 1024 * 1024


def iota(shape, dim):
    return lax.broadcasted_iota(jnp.int32, shape, dim)


def div(a, b):
    return lax.div(a, jnp.int32(b))


def rem(a, b):
    return lax.rem(a, jnp.int32(b))


def dot(a, b):
    return lax.dot_general(a, b, (((1,), (0,)), ((), ())), preferred_element_type=F32)


def dot_nt(a, b):
    return lax.dot_general(a, b, (((1,), (1,)), ((), ())), preferred_element_type=F32)


def wait_bytes(ref, sem):
    pltpu.make_async_copy(ref, ref, sem).wait()


def kernel(
    geom,
    q_ref, k_ref, v_ref, wo_ref, res_ref, gain_ref, routes_ref, gates_ref, wg_hbm, wu_hbm, wd_hbm,
    out_ref,
    abuf, arecv, wt_s, att_all, w_all, rs_send, rs_recv, res_recv, g_own, g_recv, gg_all, f_sel,
    z_send, xall, sq_acc, accg, accu, sown, e_send, e_recv, f_send, f_recv, wg_s, wu_s, wd_s,
    wsem, ssem, rsem, early, d_recv,
):
    X, Y, E, chunk_cols = geom
    PL, CTX = X * Y, 2 * X * Y
    PB = PL // E
    D = CTX * 128
    S = 2 * PL * CAP
    NCH, CE = D // chunk_cols, D // E
    tokens = CTX * 8
    key_rows = k_ref.shape[0]

    c = lax.axis_index("ctx")
    e = lax.axis_index("exp")
    x = div(c, 2 * Y)
    h = rem(div(c, Y), 2)
    y = rem(c, Y)
    p = x * Y + y
    hz = h * E + e

    def at_plane(pp):
        return div(pp, Y) * (2 * Y) + h * Y + rem(pp, Y)

    def at_z(hh):
        return x * (2 * Y) + hh * Y + y

    def send(src, dst, ssem_, rsem_, ctx, exp):
        pltpu.make_async_remote_copy(
            src_ref=src, dst_ref=dst, send_sem=ssem_, recv_sem=rsem_,
            device_id={"ctx": ctx, "exp": exp}, device_id_type=pl.DeviceIdType.MESH,
        ).start()

    barrier = pltpu.get_barrier_semaphore()

    @pl.loop(1, CTX)
    def _(i):
        pl.semaphore_signal(
            barrier, inc=1, device_id={"ctx": rem(c + i, CTX), "exp": e},
            device_id_type=pl.DeviceIdType.MESH,
        )

    @pl.loop(1, E)
    def _(i):
        for hh in range(2):
            pl.semaphore_signal(
                barrier, inc=1, device_id={"ctx": at_z(hh), "exp": rem(e + i, E)},
                device_id_type=pl.DeviceIdType.MESH,
            )

    weights = [
        pltpu.make_async_copy(a, b, wsem.at[i])
        for i, (a, b) in enumerate(((wg_hbm, wg_s), (wu_hbm, wu_s), (wd_hbm, wd_s)))
    ]
    for w in weights:
        w.start()

    lane8 = iota((8, 128), 1)
    row8 = iota((8, 128), 0)
    route = [routes_ref[:, k : k + 1] for k in range(2)]
    gate = [gates_ref[:, k : k + 1] for k in range(2)]
    hit = jnp.where((lane8 == route[0]) | (lane8 == route[1]), 1.0, 0.0)
    before = jnp.zeros((8, 128), F32)
    for t in range(7):
        before = before + jnp.where(row8 > t, hit[t : t + 1, :], 0.0)
    slot = [
        jnp.sum(jnp.where(lane8 == route[k], before, 0.0), axis=1, keepdims=True).astype(jnp.int32)
        for k in range(2)
    ]
    place = [route[k] * CAP + slot[k] for k in range(2)]
    g_own[...] = jnp.where((lane8 == place[0]) | (lane8 == place[1]), 1.0, 0.0)
    own_gates = jnp.where(lane8 == place[0], gate[0], 0.0) + jnp.where(
        lane8 == place[1], gate[1], 0.0
    )
    gg_all[pl.ds(h, 1)] = own_gates[None]
    row_s = iota((8, S), 1)
    f_sel[...] = jnp.where(
        (div(row_s, CAP) == h * PL + p) & (route[0] == e) & (slot[0] == rem(row_s, CAP)), 1.0, 0.0
    ).astype(BF16)
    w_all[pl.ds(h, 1)] = wo_ref[...][None]

    scale = 1.0 / math.sqrt(128)
    tail = key_rows - min(tokens, key_rows)

    def attend(j):
        q = q_ref[pl.ds(pl.multiple_of(j * 128, 128), 128), :]
        s = dot_nt(q, k_ref[...]) * scale
        row = j * 128 + iota((128, key_rows - tail), 0)
        token = div(row, 32) * 8 + rem(row, 8)
        limit = (CTX * key_rows - tokens) - c * key_rows + token
        masked = jnp.where(
            tail + iota((128, key_rows - tail), 1) <= limit, s[:, tail:], jnp.float32(-1e30)
        )
        s = jnp.concatenate([s[:, :tail], masked], axis=1) if tail else masked
        m = jnp.max(s, axis=1, keepdims=True)
        w = jnp.exp(s - m)
        total = jnp.sum(w, axis=1, keepdims=True)
        o = (dot(w.astype(BF16), v_ref[...]) / total).astype(BF16)
        lse = m + jnp.log(total)
        flat = jnp.sum(
            jnp.where(iota((128, 128), 0) == iota((128, 128), 1), lse, 0.0), axis=0, keepdims=True
        )
        hi = flat.astype(BF16).astype(F32)
        mid = (flat - hi).astype(BF16).astype(F32)
        lo = flat - hi - mid
        lines = jnp.where(
            row8 == 0, hi, jnp.where(row8 == 1, mid, jnp.where(row8 == 2, lo, 0.0))
        ).astype(BF16)
        for r in range(4):
            abuf[j * 4 + r, 0:32, :] = o[r * 32 : (r + 1) * 32, :]
            abuf[j * 4 + r, 32:40, :] = lines

    def send_chunk(j):
        for r in range(4):
            dest = j * 4 + r

            @pl.when(dest != c)
            def _():
                send(abuf.at[dest], arecv.at[c], ssem.at[0], rsem.at[0], dest, e)

    n_chunks = CTX // 4
    first = rem(div(c, 4) + 1, n_chunks)
    attend(first)
    pl.semaphore_wait(barrier, CTX - 1 + 2 * (E - 1))

    send(wo_ref, w_all.at[h], ssem.at[7], early.at[0], at_z(1 - h), e)
    send(gg_all.at[h], gg_all.at[h], ssem.at[8], early.at[1], at_z(1 - h), e)
    spread = div(p, PB) == e
    mine = rem(p, PB)

    @pl.when(spread)
    def _():
        @pl.loop(1, PL)
        def _(i):
            pp = rem(p + i, PL)
            there = at_plane(pp)
            low = div(pp, Y) * (2 * Y) + rem(pp, Y)
            for half in range(2):
                cols = pl.ds(pl.multiple_of((low + half * Y) * 128, 128), 128)
                send(res_ref.at[:, cols], res_recv.at[mine, half], ssem.at[9], early.at[2 + mine], there, e)
            send(g_own, g_recv.at[mine], ssem.at[10], early.at[2 + PB + mine], there, e)

        low = x * (2 * Y) + y
        for half in range(2):
            cols = pl.ds(pl.multiple_of((low + half * Y) * 128, 128), 128)
            res_recv[pl.ds(mine, 1), half] = res_ref[:, cols][None]
        g_recv[pl.ds(mine, 1)] = g_own[...][None]

    send_chunk(first)

    @pl.loop(1, n_chunks)
    def _(i):
        j = rem(first + i, n_chunks)
        attend(j)
        send_chunk(j)

    arecv[pl.ds(c, 1)] = abuf[pl.ds(c, 1)]
    wait_bytes(arecv.at[pl.ds(0, CTX - 1)], rsem.at[0])
    levels = jnp.zeros((CTX, 128), F32)
    for i in range(CTX):
        line = jnp.sum(arecv[i, 32:40, :].astype(F32), axis=0, keepdims=True)
        levels = jnp.where(iota((CTX, 128), 0) == i, line, levels)
    weight = jnp.exp(levels - jnp.max(levels, axis=0, keepdims=True))
    weight = weight / jnp.sum(weight, axis=0, keepdims=True)
    weight = jnp.concatenate([weight, jnp.zeros((128 - CTX, 128), F32)], axis=0)
    wt_s[...] = weight.T
    columns = wt_s[pl.ds(pl.multiple_of(rem(c, 4) * 32, 32), 32), :]
    attended = jnp.zeros((32, 128), F32)
    for i in range(CTX):
        attended = attended + arecv[i, 0:32, :].astype(F32) * columns[:, i : i + 1]
    att_all[pl.ds(p, 1)] = attended.astype(BF16)[None]

    @pl.loop(1, PL)
    def _(i):
        send(att_all.at[p], att_all.at[p], ssem.at[1], rsem.at[1], at_plane(rem(p + i, PL)), e)

    wait_bytes(wo_ref, early.at[0])
    projections = [
        jnp.concatenate([w_all[hh, r * 128 : (r + 1) * 128, :] for hh in range(2)], axis=1)
        for r in range(4)
    ]
    wait_bytes(att_all.at[pl.ds(0, PL - 1)], rsem.at[1])
    rows = att_all[...].reshape(PL * 32, 128)
    partial = jnp.zeros((PL, 8, 256), F32)
    for r in range(4):
        partial = partial + dot(rows, projections[r]).reshape(PL, 4, 8, 256)[:, r]
    rs_send[...] = partial.reshape(E, PB * 8, 256).astype(BF16)
    rs_recv[pl.ds(e, 1)] = rs_send[pl.ds(e, 1)]

    @pl.loop(1, E)
    def _(i):
        ee = rem(e + i, E)
        send(rs_send.at[ee], rs_recv.at[e], ssem.at[2], rsem.at[2], c, ee)

    for i in range(PB):

        @pl.when(p != e * PB + i)
        def _():
            wait_bytes(res_recv.at[i], early.at[2 + i])
            wait_bytes(g_recv.at[i], early.at[2 + PB + i])

    pick_rows = E * PB * CAP
    table = g_recv[...].reshape(PB * 8, 128).astype(BF16)
    pick = iota((pick_rows, 128), 0)
    chooser = jnp.where(
        iota((pick_rows, 128), 1) == div(pick, PB * CAP) * CAP + rem(pick, CAP), 1.0, 0.0
    ).astype(BF16)
    picks = dot_nt(chooser, table)
    pick = iota((pick_rows, PB * 8), 0)
    picks = jnp.where(
        rem(div(pick, CAP), PB) == div(iota((pick_rows, PB * 8), 1), 8), picks, 0.0
    ).astype(BF16)
    residual = jnp.concatenate(
        [
            jnp.concatenate([res_recv[i, half].astype(F32) for half in range(2)], axis=1)
            for i in range(PB)
        ],
        axis=0,
    )

    wait_bytes(rs_recv.at[pl.ds(0, E - 1)], rsem.at[2])
    stream = residual
    for i in range(E):
        stream = stream + rs_recv[i].astype(F32)
    z_send[...] = dot(picks, stream.astype(BF16)).reshape(E, PB * CAP, 256).astype(BF16)
    xall[pl.ds(p, 1), pl.ds(hz, 1)] = z_send[pl.ds(e, 1)][None]

    @pl.loop(1, 2 * E)
    def _(i):
        zz = rem(hz + i, 2 * E)
        ee = rem(zz, E)
        send(z_send.at[ee], xall.at[p, hz], ssem.at[3], rsem.at[3], at_z(div(zz, E)), ee)

    sq_acc[...] = jnp.zeros_like(sq_acc)
    accg[...] = jnp.zeros_like(accg)
    accu[...] = jnp.zeros_like(accu)
    weights[0].wait()
    weights[1].wait()
    wait_bytes(xall.at[p, pl.ds(0, 2 * E - 1)], rsem.at[3])

    @pl.loop(1, PL)
    def _(i):
        xx = rem(x + div(i, Y), X)
        yy = rem(y + rem(i, Y), Y)
        send(xall.at[p], xall.at[p], ssem.at[4], d_recv.at[i], xx * (2 * Y) + h * Y + yy, e)

    @pl.loop(0, PL)
    def _(i):
        xx = rem(x + X - div(i, Y), X)
        yy = rem(y + Y - rem(i, Y), Y)
        src = xx * Y + yy

        @pl.when(i > 0)
        def _():
            wait_bytes(xall.at[src], d_recv.at[i])

        part = xall[src].astype(F32).reshape(S, 256)
        sq_acc[...] += part[:, :128] * part[:, :128] + part[:, 128:] * part[:, 128:]
        low = pl.multiple_of((xx * (2 * Y) + yy) * 128, 128)
        high = pl.multiple_of((xx * (2 * Y) + Y + yy) * 128, 128)
        scaled = (part * gain_ref[src]).astype(BF16)
        for acc, w in ((accg, wg_s), (accu, wu_s)):
            block = jnp.concatenate([w[:, pl.ds(low, 128)], w[:, pl.ds(high, 128)]], axis=1)
            acc[...] += dot_nt(scaled, block)
        own = dot(f_sel[...], part.astype(BF16))
        sown[:, pl.ds(low, 128)] = own[:, :128]
        sown[:, pl.ds(high, 128)] = own[:, 128:]

    norm = lax.rsqrt(jnp.sum(sq_acc[...], axis=1, keepdims=True) / D + 1e-05)
    gate_val = accg[...] * norm
    act = ((gate_val / (1.0 + jnp.exp(-gate_val))) * (accu[...] * norm)).astype(BF16)
    new = iota((S, S), 0)
    order = rem(div(new, CAP), 2) * (PL * CAP) + div(new, 2 * CAP) * CAP + rem(new, CAP)
    act = dot(jnp.where(iota((S, S), 1) == order, 1.0, 0.0).astype(BF16), act).astype(BF16)

    weights[2].wait()
    for n in range(NCH):
        down = dot(act, wd_s[:, n * chunk_cols : (n + 1) * chunk_cols])
        e_send[n] = down.reshape(PL, 2 * CAP, chunk_cols).astype(BF16)
        e_recv[n, pl.ds(p, 1)] = e_send[n, pl.ds(p, 1)]

        @pl.loop(1, PL)
        def _(i):
            xx = rem(x + div(i, Y), X)
            yy = rem(y + rem(i, Y), Y)
            send(
                e_send.at[n, xx * Y + yy], e_recv.at[n, p], ssem.at[5], rsem.at[5 + n],
                xx * (2 * Y) + h * Y + yy, e,
            )

    wait_bytes(gg_all.at[h], early.at[1])
    weigh = [
        [
            jnp.sum(jnp.where(lane8 == e * CAP + s, gg_all[hh], 0.0), axis=1, keepdims=True)
            for s in range(CAP)
        ]
        for hh in range(2)
    ]
    for n in range(NCH):
        wait_bytes(e_recv.at[n, pl.ds(0, PL - 1)], rsem.at[5 + n])
        total = jnp.sum(e_recv[n].astype(F32), axis=0)
        for f in range(chunk_cols // CE):
            ee = n * (chunk_cols // CE) + f
            stream_own = sown[:, ee * CE : (ee + 1) * CE]
            for hh in range(2):
                term = jnp.where(h == hh, stream_own, 0.0)
                for s in range(CAP):
                    line = hh * CAP + s
                    term = term + weigh[hh][s] * total[line : line + 1, f * CE : (f + 1) * CE]
                f_send[hh * E + ee] = term.astype(BF16)
                away = (h != hh) | (e != ee)

                @pl.when(away)
                def _():
                    send(f_send.at[hh * E + ee], f_recv.at[hz], ssem.at[6], rsem.at[4], at_z(hh), ee)

    f_recv[pl.ds(hz, 1)] = f_send[pl.ds(hz, 1)]
    wait_bytes(f_recv.at[pl.ds(0, 2 * E - 1)], rsem.at[4])
    out_ref[...] = jnp.sum(f_recv[...].astype(F32), axis=0).astype(BF16)

    wait_bytes(abuf.at[pl.ds(0, CTX - 1)], ssem.at[0])
    wait_bytes(att_all.at[pl.ds(0, PL - 1)], ssem.at[1])
    wait_bytes(rs_send.at[pl.ds(0, E - 1)], ssem.at[2])
    wait_bytes(xall.at[0, pl.ds(0, 2 * E - 1)], ssem.at[3])
    wait_bytes(xall.at[pl.ds(0, PL - 1)], ssem.at[4])
    wait_bytes(e_send.at[:, pl.ds(0, PL - 1)], ssem.at[5])
    wait_bytes(f_send.at[pl.ds(0, 2 * E - 1)], ssem.at[6])
    wait_bytes(wo_ref, ssem.at[7])
    wait_bytes(gg_all.at[h], ssem.at[8])

    @pl.when(spread)
    def _():
        wait_bytes(f_recv.at[pl.ds(0, PL - 1), :, pl.ds(0, 256)], ssem.at[9])
        wait_bytes(f_recv.at[pl.ds(0, PL - 1), :, pl.ds(0, 256)], ssem.at[10])


def local(queries, keys, values, out_proj, residual, gain, routes, gates, w_gate, w_up, w_down):
    X, Y = PLANE
    CTX, PL, E = 2 * X * Y, X * Y, lax.axis_size("exp")
    PB, D, FF = PL // E, gain.shape[0], w_gate.shape[2]
    S, CE = 2 * PL * CAP, D // E
    chunk_cols = 1024
    NCH = D // chunk_cols
    q = queries.reshape(CTX, 8, 4, 128).transpose(0, 2, 1, 3).reshape(CTX * 32, 128)
    gains = gain.reshape(X, 2, Y, 128).transpose(0, 2, 1, 3).reshape(PL, 1, 256)
    vmem = pl.BlockSpec(memory_space=pltpu.VMEM)
    return pl.pallas_call(
        functools.partial(kernel, (X, Y, E, chunk_cols)),
        out_shape=jax.ShapeDtypeStruct((8, CE), BF16),
        in_specs=[vmem] * 8 + [pl.BlockSpec(memory_space=pl.ANY)] * 3,
        out_specs=vmem,
        scratch_shapes=[
            pltpu.VMEM((CTX, 40, 128), BF16),
            pltpu.VMEM((CTX, 40, 128), BF16),
            pltpu.VMEM((128, 128), F32),
            pltpu.VMEM((PL, 32, 128), BF16),
            pltpu.VMEM((2, 512, 128), BF16),
            pltpu.VMEM((E, PB * 8, 256), BF16),
            pltpu.VMEM((E, PB * 8, 256), BF16),
            pltpu.VMEM((PB, 2, 8, 128), BF16),
            pltpu.VMEM((8, 128), F32),
            pltpu.VMEM((PB, 8, 128), F32),
            pltpu.VMEM((2, 8, 128), F32),
            pltpu.VMEM((8, S), BF16),
            pltpu.VMEM((E, PB * CAP, 256), BF16),
            pltpu.VMEM((PL, 2 * E, PB * CAP, 256), BF16),
            pltpu.VMEM((S, 128), F32),
            pltpu.VMEM((S, FF), F32),
            pltpu.VMEM((S, FF), F32),
            pltpu.VMEM((8, D), F32),
            pltpu.VMEM((NCH, PL, 2 * CAP, chunk_cols), BF16),
            pltpu.VMEM((NCH, PL, 2 * CAP, chunk_cols), BF16),
            pltpu.VMEM((2 * E, 8, CE), BF16),
            pltpu.VMEM((2 * E, 8, CE), BF16),
            pltpu.VMEM((FF, D), BF16),
            pltpu.VMEM((FF, D), BF16),
            pltpu.VMEM((FF, D), BF16),
            pltpu.SemaphoreType.DMA((3,)),
            pltpu.SemaphoreType.DMA((11,)),
            pltpu.SemaphoreType.DMA((5 + NCH,)),
            pltpu.SemaphoreType.DMA((2 + 2 * PB,)),
            pltpu.SemaphoreType.DMA((PL,)),
        ],
        compiler_params=pltpu.CompilerParams(
            collective_id=0, has_side_effects=True, vmem_limit_bytes=VMEM_LIMIT
        ),
    )(
        q,
        keys.reshape(keys.shape[0], 128),
        values.reshape(values.shape[0], 128),
        out_proj,
        residual,
        gains,
        routes,
        gates,
        jnp.swapaxes(w_gate, 1, 2).reshape(FF, D),
        jnp.swapaxes(w_up, 1, 2).reshape(FF, D),
        w_down.reshape(FF, D),
    )


def solution(mesh):
    return jax.shard_map(
        local,
        mesh=mesh,
        in_specs=(
            P(None, "exp", None),
            P("ctx", "exp", None),
            P("ctx", "exp", None),
            P("exp", "ctx"),
            P("ctx", None),
            P(),
            P("ctx", None),
            P("ctx", None),
            P("exp", None, "ctx"),
            P("exp", None, "ctx"),
            P("exp", "ctx", None),
        ),
        out_specs=P("ctx", "exp"),
        check_vma=False,
    )
```

time: 1040 us -> 88.7 us (0.09)
  waiting for transfers between devices: 690 us -> 0 us
  blocking collectives: 216 us -> 0 us
  Pallas kernels: 0 us -> 80.4 us
  other arithmetic: 47.1 us -> 0 us
  local copies, waits for them, and re-layouts: 48.1 us -> 6.99 us
  matrix products: 22.4 us -> 0 us
  between operations: 14.3 us -> 0.01 us
    unnamed x7 -> x0, waiting for transfers between devices: 401 us -> none
    all_gather x2 -> x0, blocking collectives: 216 us -> none  [joined(): gathered = jax.tree.map(lambda a: lax.all_gather(a, axis), part)]
    all_gather x3 -> x0, waiting for transfers between devices: 171 us -> none  [the longest x1 92.7 us: local(): shard_rows = lax.all_gather(buffer, 'ctx', axis=0, tiled=True)]
    pallas_call x0 -> x1, Pallas kernels: none -> 80.4 us  [local(): pl.pallas_call(functools.partial(kernel, (X, Y, E, chunk_cols)), out_shap...]
    psum x1 -> x0, waiting for transfers between devices: 63.3 us -> none  [local(): lax.psum(partial_value.astype(jnp.bfloat16), 'exp').astype(jnp.float32)]
    reduce_scatter x1 -> x0, waiting for transfers between devices: 54.6 us -> none  [local(): lax.psum_scatter(contribution.astype(jnp.bfloat16), 'exp', scatter_dimens...]
    add x34 -> x0, other arithmetic: 40.3 us -> none  [the longest x31 39.3 us: combine_parts(): first_part[2] * first_scale[..., None]]
    dynamic_slice x32 -> x0, local copies, waits for them, and re-layouts: 33.8 us -> none  [the longest x31 33.8 us: take(): lax.dynamic_index_in_dim(a, source, 0, False)]
  transfers between devices with their start and end apart: 6 -> 0, of which waited for: 6 -> 0; matrix products, arithmetic and copies ran while one was open for 9% -> 0% of each run, Pallas kernels for 0% -> 0%
where the time goes in v1:
time: 88.7 us; the launch traced here: 87.4 us
  Pallas kernels  80.4 us (91%)
  local copies, waits for them, and re-layouts  6.99 us (8%)
    pallas_call x1, Pallas kernels, local(): pl.pallas_call(functools.partial(kernel, (X, Y, E, chunk_cols)), out_shap...  80.4 us
    unnamed x3, local copies, waits for them, and re-layouts  3.99 us

profile of v1, /device:TPU:1, one launch (start us, length us, event | category | flops | bytes accessed | tf_op | source)
XLA Modules:
  0.0 87.4 jit_solution(13041072320159630537)
XLA Ops:
  0.0 1.3 %copy.17.routes_ref = s32[8,2]{1,0:T(8,128)} copy(s32[8,2]{0,1:T(2,128)} %param.17) | data formatting | bytes 128 | tf_op args[6]
  1.3 1.3 %copy.18.gates_ref = f32[8,2]{1,0:T(8,128)} copy(f32[8,2]{0,1:T(2,128)} %param.18) | data formatting | bytes 128 | tf_op args[7]
  2.7 1.3 %copy.16 = f32[4,4,2,128]{3,2,1,0:T(2,128)} copy(f32[4,4,2,128]{3,1,2,0:T(4,128)} %bitcast.25) | data formatting | bytes 32768 | tf_op jit(solution)/shard_map/transpose | solution.py:390
  4.0 1.7 %copy.15 = bf16[32,8,4,128]{3,1,2,0:T(8,128)(2,1)} copy(bf16[32,8,4,128]{3,2,1,0:T(4,128)(2,1)} %bitcast.23) | data formatting | bytes 524288 | tf_op jit(solution)/shard_map/reshape | solution.py:389
  5.7 80.4 %shard_map.109 = bf16[8,512]{1,0:T(8,128)(2,1)} custom-call(bf16[1024,128]{1,0:T(8,128)(2,1)} %bitcast.20, bf16[1024,128]{1,0:T(8,128)(2,1)} %bitcast.21, bf16[1024,128]{1,0:T(8,128)(2,1)} %bitcast.22, bf16[512,128]{1,0:T(8,128)(2,1)} %wo_ref.1, bf16[8,4096]{1,0:T(8,128)(2,1)} %res_ref.1, f32[16,1,256]{2,1,0:T(1,128)} %bitcast.24, s32[8,2]{1,0:T(8,128)} %copy.17.routes_ref, ...), custom_call_target="tpu_custom_call" | custom-call | tf_op jit(solution)/shard_map/pallas_call | solution.py:392
  86.1 1.3 %copy.20 = bf16[8,512]{1,0:T(8,128)(2,1)} copy(bf16[8,512]{1,0:T(8,128)(2,1)} %shard_map.109) | data formatting | bytes 16384

commit v2 on v1

--- a/solution.py
+++ b/solution.py
@@ -35,6 +35,10 @@
     return lax.dot_general(a, b, (((1,), (1,)), ((), ())), preferred_element_type=F32)
 
 
+def near_first(n):
+    return sorted(range(1, n), key=lambda i: min(i, n - i))
+
+
 def wait_bytes(ref, sem):
     pltpu.make_async_copy(ref, ref, sem).wait()
 
@@ -44,8 +48,9 @@
     q_ref, k_ref, v_ref, wo_ref, res_ref, gain_ref, routes_ref, gates_ref, wg_hbm, wu_hbm, wd_hbm,
     out_ref,
     abuf, arecv, wt_s, att_all, w_all, rs_send, rs_recv, res_recv, g_own, g_recv, gg_all, f_sel,
-    z_send, xall, sq_acc, accg, accu, sown, e_send, e_recv, f_send, f_recv, wg_s, wu_s, wd_s,
-    wsem, ssem, rsem, early, d_recv,
+    z_send, xall, sq_acc, accg, accu, sown, e_send, e_recv, t_send, t_recv, f_send, f_recv,
+    wg_s, wu_s, wd_s,
+    wsem, ssem, rsem, early, d_recv, e_sem, t_sem,
 ):
     X, Y, E, chunk_cols = geom
     PL, CTX = X * Y, 2 * X * Y
@@ -102,8 +107,17 @@
 
     lane8 = iota((8, 128), 1)
     row8 = iota((8, 128), 0)
-    route = [routes_ref[:, k : k + 1] for k in range(2)]
-    gate = [gates_ref[:, k : k + 1] for k in range(2)]
+    diagonal = iota((8, 8), 0) == iota((8, 8), 1)
+    route = [
+        jnp.sum(
+            jnp.where(diagonal, routes_ref[k : k + 1, :].astype(F32), 0.0), axis=1, keepdims=True
+        ).astype(jnp.int32)
+        for k in range(2)
+    ]
+    gate = [
+        jnp.sum(jnp.where(diagonal, gates_ref[k : k + 1, :], 0.0), axis=1, keepdims=True)
+        for k in range(2)
+    ]
     hit = jnp.where((lane8 == route[0]) | (lane8 == route[1]), 1.0, 0.0)
     before = jnp.zeros((8, 128), F32)
     for t in range(7):
@@ -131,7 +145,7 @@
         q = q_ref[pl.ds(pl.multiple_of(j * 128, 128), 128), :]
         s = dot_nt(q, k_ref[...]) * scale
         row = j * 128 + iota((128, key_rows - tail), 0)
-        token = div(row, 32) * 8 + rem(row, 8)
+        token = div(row, 4)
         limit = (CTX * key_rows - tokens) - c * key_rows + token
         masked = jnp.where(
             tail + iota((128, key_rows - tail), 1) <= limit, s[:, tail:], jnp.float32(-1e30)
@@ -168,7 +182,6 @@
     attend(first)
     pl.semaphore_wait(barrier, CTX - 1 + 2 * (E - 1))
 
-    send(wo_ref, w_all.at[h], ssem.at[7], early.at[0], at_z(1 - h), e)
     send(gg_all.at[h], gg_all.at[h], ssem.at[8], early.at[1], at_z(1 - h), e)
     spread = div(p, PB) == e
     mine = rem(p, PB)
@@ -198,6 +211,8 @@
         j = rem(first + i, n_chunks)
         attend(j)
         send_chunk(j)
+
+    send(wo_ref, w_all.at[h], ssem.at[7], early.at[0], at_z(1 - h), e)
 
     arecv[pl.ds(c, 1)] = abuf[pl.ds(c, 1)]
     wait_bytes(arecv.at[pl.ds(0, CTX - 1)], rsem.at[0])
@@ -213,27 +228,27 @@
     attended = jnp.zeros((32, 128), F32)
     for i in range(CTX):
         attended = attended + arecv[i, 0:32, :].astype(F32) * columns[:, i : i + 1]
-    att_all[pl.ds(p, 1)] = attended.astype(BF16)[None]
-
-    @pl.loop(1, PL)
-    def _(i):
-        send(att_all.at[p], att_all.at[p], ssem.at[1], rsem.at[1], at_plane(rem(p + i, PL)), e)
+    new = iota((32, 32), 0)
+    order = rem(new, 8) * 4 + div(new, 8)
+    swap = jnp.where(iota((32, 32), 1) == order, 1.0, 0.0).astype(BF16)
+    heads = dot(swap, attended.astype(BF16)).reshape(4, 1, 8, 128)
+    att_all[:, pl.ds(p, 1)] = heads.astype(BF16)
+    for i in range(X):
+        for j in range(Y):
+            if i or j:
+                there = rem(x + i, X) * (2 * Y) + h * Y + rem(y + j, Y)
+                send(att_all.at[:, p], att_all.at[:, p], ssem.at[1], rsem.at[1], there, e)
 
     wait_bytes(wo_ref, early.at[0])
-    projections = [
-        jnp.concatenate([w_all[hh, r * 128 : (r + 1) * 128, :] for hh in range(2)], axis=1)
-        for r in range(4)
-    ]
-    wait_bytes(att_all.at[pl.ds(0, PL - 1)], rsem.at[1])
-    rows = att_all[...].reshape(PL * 32, 128)
-    partial = jnp.zeros((PL, 8, 256), F32)
-    for r in range(4):
-        partial = partial + dot(rows, projections[r]).reshape(PL, 4, 8, 256)[:, r]
+    wait_bytes(att_all.at[:, pl.ds(0, PL - 1)], rsem.at[1])
+    rows = jnp.concatenate(
+        [att_all[r].astype(F32).reshape(PL * 8, 128) for r in range(4)], axis=1
+    ).astype(BF16)
+    partial = dot(rows, jnp.concatenate([w_all[0], w_all[1]], axis=1))
     rs_send[...] = partial.reshape(E, PB * 8, 256).astype(BF16)
     rs_recv[pl.ds(e, 1)] = rs_send[pl.ds(e, 1)]
 
-    @pl.loop(1, E)
-    def _(i):
+    for i in range(1, E):
         ee = rem(e + i, E)
         send(rs_send.at[ee], rs_recv.at[e], ssem.at[2], rsem.at[2], c, ee)
 
@@ -270,8 +285,7 @@
     z_send[...] = dot(picks, stream.astype(BF16)).reshape(E, PB * CAP, 256).astype(BF16)
     xall[pl.ds(p, 1), pl.ds(hz, 1)] = z_send[pl.ds(e, 1)][None]
 
-    @pl.loop(1, 2 * E)
-    def _(i):
+    for i in range(1, 2 * E):
         zz = rem(hz + i, 2 * E)
         ee = rem(zz, E)
         send(z_send.at[ee], xall.at[p, hz], ssem.at[3], rsem.at[3], at_z(div(zz, E)), ee)
@@ -283,27 +297,22 @@
     weights[1].wait()
     wait_bytes(xall.at[p, pl.ds(0, 2 * E - 1)], rsem.at[3])
 
-    @pl.loop(1, PL)
-    def _(i):
-        xx = rem(x + div(i, Y), X)
-        yy = rem(y + rem(i, Y), Y)
-        send(xall.at[p], xall.at[p], ssem.at[4], d_recv.at[i], xx * (2 * Y) + h * Y + yy, e)
-
-    @pl.loop(0, PL)
-    def _(i):
-        xx = rem(x + X - div(i, Y), X)
-        yy = rem(y + Y - rem(i, Y), Y)
+    def ctx_of(i, j):
+        return rem(x + i, X) * (2 * Y) + h * Y + rem(y + j, Y)
+
+    def source(i, j):
+        return rem(x + X - i, X), rem(y + Y - j, Y)
+
+    low_half, high_half = pl.ds(0, E), pl.ds(E, E)
+
+    def expert_products(xx, yy):
         src = xx * Y + yy
-
-        @pl.when(i > 0)
-        def _():
-            wait_bytes(xall.at[src], d_recv.at[i])
-
         part = xall[src].astype(F32).reshape(S, 256)
         sq_acc[...] += part[:, :128] * part[:, :128] + part[:, 128:] * part[:, 128:]
         low = pl.multiple_of((xx * (2 * Y) + yy) * 128, 128)
         high = pl.multiple_of((xx * (2 * Y) + Y + yy) * 128, 128)
-        scaled = (part * gain_ref[src]).astype(BF16)
+        gain = [gain_ref[pl.ds(xx * (2 * Y) + half * Y + yy, 1), :] for half in range(2)]
+        scaled = (part * jnp.concatenate(gain, axis=1)).astype(BF16)
         for acc, w in ((accg, wg_s), (accu, wu_s)):
             block = jnp.concatenate([w[:, pl.ds(low, 128)], w[:, pl.ds(high, 128)]], axis=1)
             acc[...] += dot_nt(scaled, block)
@@ -311,6 +320,45 @@
         sown[:, pl.ds(low, 128)] = own[:, :128]
         sown[:, pl.ds(high, 128)] = own[:, 128:]
 
+    for i in near_first(max(X, Y)):
+        if i < X:
+            send(xall.at[p], xall.at[p], ssem.at[4], d_recv.at[i * Y], ctx_of(i, 0), e)
+        if i < Y:
+            send(xall.at[p], xall.at[p], ssem.at[4], d_recv.at[i], ctx_of(0, i), e)
+    expert_products(x, y)
+    for i in near_first(max(X, Y)):
+        if i < X:
+            xx, yy = source(i, 0)
+            src = xx * Y + yy
+            wait_bytes(xall.at[src], d_recv.at[i * Y])
+            for j in near_first(Y):
+                half = xall.at[src, low_half]
+                send(half, half, ssem.at[4], d_recv.at[i * Y + j], ctx_of(0, j), e)
+        if i < Y:
+            xx, yy = source(0, i)
+            src = xx * Y + yy
+            wait_bytes(xall.at[src], d_recv.at[i])
+            for j in near_first(X):
+                half = xall.at[src, high_half]
+                send(half, half, ssem.at[4], d_recv.at[PL + j * Y + i], ctx_of(j, 0), e)
+
+    @pl.loop(1, X)
+    def _(i):
+        expert_products(*source(i, 0))
+
+    @pl.loop(1, Y)
+    def _(i):
+        expert_products(*source(0, i))
+
+    @pl.loop(0, (X - 1) * (Y - 1))
+    def _(t):
+        i, j = div(t, Y - 1) + 1, rem(t, Y - 1) + 1
+        xx, yy = source(i, j)
+        src = xx * Y + yy
+        wait_bytes(xall.at[src, low_half], d_recv.at[i * Y + j])
+        wait_bytes(xall.at[src, high_half], d_recv.at[PL + i * Y + j])
+        expert_products(xx, yy)
+
     norm = lax.rsqrt(jnp.sum(sq_acc[...], axis=1, keepdims=True) / D + 1e-05)
     gate_val = accg[...] * norm
     act = ((gate_val / (1.0 + jnp.exp(-gate_val))) * (accu[...] * norm)).astype(BF16)
@@ -321,17 +369,35 @@
     weights[2].wait()
     for n in range(NCH):
         down = dot(act, wd_s[:, n * chunk_cols : (n + 1) * chunk_cols])
-        e_send[n] = down.reshape(PL, 2 * CAP, chunk_cols).astype(BF16)
-        e_recv[n, pl.ds(p, 1)] = e_send[n, pl.ds(p, 1)]
-
-        @pl.loop(1, PL)
-        def _(i):
-            xx = rem(x + div(i, Y), X)
-            yy = rem(y + rem(i, Y), Y)
-            send(
-                e_send.at[n, xx * Y + yy], e_recv.at[n, p], ssem.at[5], rsem.at[5 + n],
-                xx * (2 * Y) + h * Y + yy, e,
-            )
+        e_send[n] = down.reshape(X, Y, 2 * CAP, chunk_cols).astype(BF16)
+        if n % 2 == 0:
+            for j in near_first(Y):
+                block = e_send.at[n, :, rem(y + j, Y)]
+                send(block, e_recv.at[n, j - 1, pl.ds(0, X)], ssem.at[5], e_sem.at[n], ctx_of(0, j), e)
+        else:
+            for i in near_first(X):
+                block = e_send.at[n, rem(x + i, X)]
+                send(block, e_recv.at[n, i - 1, pl.ds(0, Y)], ssem.at[11], e_sem.at[n], ctx_of(i, 0), e)
+
+    for n in range(NCH):
+        if n % 2 == 0:
+            wait_bytes(e_recv.at[n, pl.ds(0, Y - 1), pl.ds(0, X)], e_sem.at[n])
+            line = e_send[n, :, pl.ds(y, 1)].reshape(X, 2 * CAP, chunk_cols).astype(F32)
+            for j in range(Y - 1):
+                line = line + e_recv[n, j, :X].astype(F32)
+            t_send[n, :X] = line.astype(BF16)
+            for i in near_first(X):
+                block = t_send.at[n, rem(x + i, X)]
+                send(block, t_recv.at[n, i - 1], ssem.at[12], t_sem.at[n], ctx_of(i, 0), e)
+        else:
+            wait_bytes(e_recv.at[n, pl.ds(0, X - 1), pl.ds(0, Y)], e_sem.at[n])
+            line = e_send[n, pl.ds(x, 1)].reshape(Y, 2 * CAP, chunk_cols).astype(F32)
+            for i in range(X - 1):
+                line = line + e_recv[n, i, :Y].astype(F32)
+            t_send[n, :Y] = line.astype(BF16)
+            for j in near_first(Y):
+                block = t_send.at[n, rem(y + j, Y)]
+                send(block, t_recv.at[n, j - 1], ssem.at[13], t_sem.at[n], ctx_of(0, j), e)
 
     wait_bytes(gg_all.at[h], early.at[1])
     weigh = [
@@ -342,8 +408,11 @@
         for hh in range(2)
     ]
     for n in range(NCH):
-        wait_bytes(e_recv.at[n, pl.ds(0, PL - 1)], rsem.at[5 + n])
-        total = jnp.sum(e_recv[n].astype(F32), axis=0)
+        peers, mine = (X - 1, x) if n % 2 == 0 else (Y - 1, y)
+        wait_bytes(t_recv.at[n, pl.ds(0, peers)], t_sem.at[n])
+        total = t_send[n, mine].astype(F32)
+        for i in range(peers):
+            total = total + t_recv[n, i].astype(F32)
         for f in range(chunk_cols // CE):
             ee = n * (chunk_cols // CE) + f
             stream_own = sown[:, ee * CE : (ee + 1) * CE]
@@ -364,11 +433,15 @@
     out_ref[...] = jnp.sum(f_recv[...].astype(F32), axis=0).astype(BF16)
 
     wait_bytes(abuf.at[pl.ds(0, CTX - 1)], ssem.at[0])
-    wait_bytes(att_all.at[pl.ds(0, PL - 1)], ssem.at[1])
+    wait_bytes(att_all.at[:, pl.ds(0, PL - 1)], ssem.at[1])
     wait_bytes(rs_send.at[pl.ds(0, E - 1)], ssem.at[2])
     wait_bytes(xall.at[0, pl.ds(0, 2 * E - 1)], ssem.at[3])
     wait_bytes(xall.at[pl.ds(0, PL - 1)], ssem.at[4])
-    wait_bytes(e_send.at[:, pl.ds(0, PL - 1)], ssem.at[5])
+    even, odd = pl.ds(0, (NCH + 1) // 2), pl.ds(0, NCH // 2)
+    wait_bytes(e_send.at[even, :, pl.ds(0, Y - 1)], ssem.at[5])
+    wait_bytes(e_send.at[odd, pl.ds(0, X - 1)], ssem.at[11])
+    wait_bytes(t_send.at[even, pl.ds(0, X - 1)], ssem.at[12])
+    wait_bytes(t_send.at[odd, pl.ds(0, Y - 1)], ssem.at[13])
     wait_bytes(f_send.at[pl.ds(0, 2 * E - 1)], ssem.at[6])
     wait_bytes(wo_ref, ssem.at[7])
     wait_bytes(gg_all.at[h], ssem.at[8])
@@ -384,10 +457,8 @@
     CTX, PL, E = 2 * X * Y, X * Y, lax.axis_size("exp")
     PB, D, FF = PL // E, gain.shape[0], w_gate.shape[2]
     S, CE = 2 * PL * CAP, D // E
-    chunk_cols = 1024
+    chunk_cols, side = 1024, max(X, Y)
     NCH = D // chunk_cols
-    q = queries.reshape(CTX, 8, 4, 128).transpose(0, 2, 1, 3).reshape(CTX * 32, 128)
-    gains = gain.reshape(X, 2, Y, 128).transpose(0, 2, 1, 3).reshape(PL, 1, 256)
     vmem = pl.BlockSpec(memory_space=pltpu.VMEM)
     return pl.pallas_call(
         functools.partial(kernel, (X, Y, E, chunk_cols)),
@@ -398,7 +469,7 @@
             pltpu.VMEM((CTX, 40, 128), BF16),
             pltpu.VMEM((CTX, 40, 128), BF16),
             pltpu.VMEM((128, 128), F32),
-            pltpu.VMEM((PL, 32, 128), BF16),
+            pltpu.VMEM((4, PL, 8, 128), BF16),
             pltpu.VMEM((2, 512, 128), BF16),
             pltpu.VMEM((E, PB * 8, 256), BF16),
             pltpu.VMEM((E, PB * 8, 256), BF16),
@@ -413,31 +484,35 @@
             pltpu.VMEM((S, FF), F32),
             pltpu.VMEM((S, FF), F32),
             pltpu.VMEM((8, D), F32),
-            pltpu.VMEM((NCH, PL, 2 * CAP, chunk_cols), BF16),
-            pltpu.VMEM((NCH, PL, 2 * CAP, chunk_cols), BF16),
+            pltpu.VMEM((NCH, X, Y, 2 * CAP, chunk_cols), BF16),
+            pltpu.VMEM((NCH, side - 1, side, 2 * CAP, chunk_cols), BF16),
+            pltpu.VMEM((NCH, side, 2 * CAP, chunk_cols), BF16),
+            pltpu.VMEM((NCH, side - 1, 2 * CAP, chunk_cols), BF16),
             pltpu.VMEM((2 * E, 8, CE), BF16),
             pltpu.VMEM((2 * E, 8, CE), BF16),
             pltpu.VMEM((FF, D), BF16),
             pltpu.VMEM((FF, D), BF16),
             pltpu.VMEM((FF, D), BF16),
             pltpu.SemaphoreType.DMA((3,)),
-            pltpu.SemaphoreType.DMA((11,)),
-            pltpu.SemaphoreType.DMA((5 + NCH,)),
+            pltpu.SemaphoreType.DMA((14,)),
+            pltpu.SemaphoreType.DMA((5,)),
             pltpu.SemaphoreType.DMA((2 + 2 * PB,)),
-            pltpu.SemaphoreType.DMA((PL,)),
+            pltpu.SemaphoreType.DMA((2 * PL,)),
+            pltpu.SemaphoreType.DMA((NCH,)),
+            pltpu.SemaphoreType.DMA((NCH,)),
         ],
         compiler_params=pltpu.CompilerParams(
             collective_id=0, has_side_effects=True, vmem_limit_bytes=VMEM_LIMIT
         ),
     )(
-        q,
+        queries.reshape(CTX * 32, 128),
         keys.reshape(keys.shape[0], 128),
         values.reshape(values.shape[0], 128),
         out_proj,
         residual,
-        gains,
-        routes,
-        gates,
+        gain.reshape(CTX, 128),
+        routes.T,
+        gates.T,
         jnp.swapaxes(w_gate, 1, 2).reshape(FF, D),
         jnp.swapaxes(w_up, 1, 2).reshape(FF, D),
         w_down.reshape(FF, D),

time: 88.7 us -> 72.4 us (0.82); the launches traced: 87.4 us -> 72.2 us
  Pallas kernels: 80.4 us -> 70.9 us
  local copies, waits for them, and re-layouts: 6.99 us -> 1.3 us
    pallas_call x1, Pallas kernels: 80.4 us -> 70.9 us  [local(): pl.pallas_call(functools.partial(kernel, (X, Y, E, chunk_cols)), out_shap...]
    unnamed x3 -> x1, local copies, waits for them, and re-layouts: 3.99 us -> 1.3 us
    reshape x1 -> x0, local copies, waits for them, and re-layouts: 1.68 us -> none  [local(): queries.reshape(CTX, 8, 4, 128).transpose(0, 2, 1, 3).reshape(CTX * 32, 128)]
    transpose x1 -> x0, local copies, waits for them, and re-layouts: 1.32 us -> none  [local(): gains = gain.reshape(X, 2, Y, 128).transpose(0, 2, 1, 3).reshape(PL, 1, 256)]
where the time goes in v2:
time: 72.4 us; the launch traced here: 72.2 us
  Pallas kernels  70.9 us (98%)
  local copies, waits for them, and re-layouts  1.3 us (2%)
    pallas_call x1, Pallas kernels, local(): pl.pallas_call(functools.partial(kernel, (X, Y, E, chunk_cols)), out_shap...  70.9 us

profile of v2, /device:TPU:1, one launch (start us, length us, event | category | flops | bytes accessed | tf_op | source)
XLA Modules:
  0.0 72.2 jit_solution(12356008647330346615)
XLA Ops:
  0.0 70.9 %shard_map.109 = bf16[8,512]{1,0:T(8,128)(2,1)} custom-call(bf16[1024,128]{1,0:T(8,128)(2,1)} %bitcast.16, bf16[1024,128]{1,0:T(8,128)(2,1)} %bitcast.17, bf16[1024,128]{1,0:T(8,128)(2,1)} %bitcast.18, bf16[512,128]{1,0:T(8,128)(2,1)} %wo_ref.1, bf16[8,4096]{1,0:T(8,128)(2,1)} %res_ref.1, f32[32,128]{1,0:T(8,128)} %bitcast.19, s32[2,8]{1,0:T(2,128)} %bitcast.20, ...), custom_call_target="tpu_custom_call" | custom-call | tf_op jit(solution)/shard_map/pallas_call | solution.py:463
  70.9 1.3 %copy.13 = bf16[8,512]{1,0:T(8,128)(2,1)} copy(bf16[8,512]{1,0:T(8,128)(2,1)} %shard_map.109) | data formatting | bytes 16384

commit v3 on v2

--- a/solution.py
+++ b/solution.py
@@ -27,6 +27,11 @@
     return lax.rem(a, jnp.int32(b))
 
 
+def parts(a, n):
+    assert n & (n - 1) == 0
+    return lax.shift_right_logical(a, jnp.int32(n.bit_length() - 1)), a & (n - 1)
+
+
 def dot(a, b):
     return lax.dot_general(a, b, (((1,), (0,)), ((), ())), preferred_element_type=F32)
 
@@ -45,12 +50,13 @@
 
 def kernel(
     geom,
-    q_ref, k_ref, v_ref, wo_ref, res_ref, gain_ref, routes_ref, gates_ref, wg_hbm, wu_hbm, wd_hbm,
-    out_ref,
-    abuf, arecv, wt_s, att_all, w_all, rs_send, rs_recv, res_recv, g_own, g_recv, gg_all, f_sel,
+    q_hbm, k_hbm, v_hbm, wo_hbm, res_hbm, gain_hbm, routes_hbm, gates_hbm, wg_hbm, wu_hbm, wd_hbm,
+    out_hbm,
+    out_s, q_ref, k_ref, v_ref, res_ref, gain_ref, routes_ref, gates_ref, swap_s, order_s, picks_s, mask_s,
+    abuf, arecv, a_out, a_in, wt_s, att_all, w_all, rs_send, rs_recv, res_recv, g_own, g_recv, gg_all, f_sel,
     z_send, xall, sq_acc, accg, accu, sown, e_send, e_recv, t_send, t_recv, f_send, f_recv,
     wg_s, wu_s, wd_s,
-    wsem, ssem, rsem, early, d_recv, e_sem, t_sem,
+    wsem, ssem, a_sem, rsem, early, d_recv, e_sem, t_sem,
 ):
     X, Y, E, chunk_cols = geom
     PL, CTX = X * Y, 2 * X * Y
@@ -83,27 +89,53 @@
 
     barrier = pltpu.get_barrier_semaphore()
 
-    @pl.loop(1, CTX)
-    def _(i):
-        pl.semaphore_signal(
-            barrier, inc=1, device_id={"ctx": rem(c + i, CTX), "exp": e},
-            device_id_type=pl.DeviceIdType.MESH,
-        )
-
-    @pl.loop(1, E)
-    def _(i):
+    for i in range(X):
+        for hh in range(2):
+            for j in range(Y):
+                there = rem(x + i, X) * (2 * Y) + rem(h + hh, 2) * Y + rem(y + j, Y)
+                if i or hh or j:
+                    pl.semaphore_signal(
+                        barrier, inc=1, device_id={"ctx": there, "exp": e},
+                        device_id_type=pl.DeviceIdType.MESH,
+                    )
+    for i in range(1, E):
         for hh in range(2):
             pl.semaphore_signal(
                 barrier, inc=1, device_id={"ctx": at_z(hh), "exp": rem(e + i, E)},
                 device_id_type=pl.DeviceIdType.MESH,
             )
 
-    weights = [
+    fetches = [
         pltpu.make_async_copy(a, b, wsem.at[i])
-        for i, (a, b) in enumerate(((wg_hbm, wg_s), (wu_hbm, wu_s), (wd_hbm, wd_s)))
+        for i, (a, b) in enumerate((
+            (wg_hbm, wg_s), (wu_hbm, wu_s), (wd_hbm, wd_s),
+            (q_hbm, q_ref), (k_hbm, k_ref), (v_hbm, v_ref), (routes_hbm, routes_ref),
+            (gates_hbm, gates_ref), (res_hbm, res_ref), (gain_hbm, gain_ref), (wo_hbm, w_all.at[h]),
+        ))
     ]
-    for w in weights:
-        w.start()
+    for i in (6, 7, 3, 4, 5, 8, 9, 10, 0, 1, 2):
+        fetches[i].start()
+    weights = fetches[:3]
+
+    new, old = iota((32, 32), 0), iota((32, 32), 1)
+    head, token = parts(new, 8)
+    swap_s[...] = jnp.where(old == token * 4 + head, 1.0, 0.0).astype(BF16)
+    high, s4 = parts(iota((S, S), 0), CAP)
+    plane, zz = parts(high, 2)
+    order_s[...] = jnp.where(
+        iota((S, S), 1) == zz * (PL * CAP) + plane * CAP + s4, 1.0, 0.0
+    ).astype(BF16)
+    pick_rows = E * PB * CAP
+    high, s4 = parts(iota((pick_rows, 128), 0), CAP)
+    picks_s[...] = jnp.where(
+        iota((pick_rows, 128), 1) == parts(high, PB)[0] * CAP + s4, 1.0, 0.0
+    ).astype(BF16)
+    high, _ = parts(iota((pick_rows, PB * 8), 0), CAP)
+    mask_s[...] = jnp.where(
+        parts(high, PB)[1] == parts(iota((pick_rows, PB * 8), 1), 8)[0], 1.0, 0.0
+    )
+    fetches[6].wait()
+    fetches[7].wait()
 
     lane8 = iota((8, 128), 1)
     row8 = iota((8, 128), 0)
@@ -133,19 +165,26 @@
     )
     gg_all[pl.ds(h, 1)] = own_gates[None]
     row_s = iota((8, S), 1)
+    high, s4 = parts(row_s, CAP)
     f_sel[...] = jnp.where(
-        (div(row_s, CAP) == h * PL + p) & (route[0] == e) & (slot[0] == rem(row_s, CAP)), 1.0, 0.0
+        (high == h * PL + p) & (route[0] == e) & (slot[0] == s4), 1.0, 0.0
     ).astype(BF16)
-    w_all[pl.ds(h, 1)] = wo_ref[...][None]
 
     scale = 1.0 / math.sqrt(128)
     tail = key_rows - min(tokens, key_rows)
+
+    def level_lines(flat):
+        hi = flat.astype(BF16).astype(F32)
+        mid = (flat - hi).astype(BF16).astype(F32)
+        lo = flat - hi - mid
+        return jnp.where(
+            row8 == 0, hi, jnp.where(row8 == 1, mid, jnp.where(row8 == 2, lo, 0.0))
+        ).astype(BF16)
 
     def attend(j):
         q = q_ref[pl.ds(pl.multiple_of(j * 128, 128), 128), :]
         s = dot_nt(q, k_ref[...]) * scale
-        row = j * 128 + iota((128, key_rows - tail), 0)
-        token = div(row, 4)
+        token = j * 32 + parts(iota((128, key_rows - tail), 0), 4)[0]
         limit = (CTX * key_rows - tokens) - c * key_rows + token
         masked = jnp.where(
             tail + iota((128, key_rows - tail), 1) <= limit, s[:, tail:], jnp.float32(-1e30)
@@ -159,28 +198,37 @@
         flat = jnp.sum(
             jnp.where(iota((128, 128), 0) == iota((128, 128), 1), lse, 0.0), axis=0, keepdims=True
         )
-        hi = flat.astype(BF16).astype(F32)
-        mid = (flat - hi).astype(BF16).astype(F32)
-        lo = flat - hi - mid
-        lines = jnp.where(
-            row8 == 0, hi, jnp.where(row8 == 1, mid, jnp.where(row8 == 2, lo, 0.0))
-        ).astype(BF16)
+        lines = level_lines(flat)
         for r in range(4):
             abuf[j * 4 + r, 0:32, :] = o[r * 32 : (r + 1) * 32, :]
             abuf[j * 4 + r, 32:40, :] = lines
 
-    def send_chunk(j):
-        for r in range(4):
-            dest = j * 4 + r
-
-            @pl.when(dest != c)
-            def _():
-                send(abuf.at[dest], arecv.at[c], ssem.at[0], rsem.at[0], dest, e)
-
-    n_chunks = CTX // 4
-    first = rem(div(c, 4) + 1, n_chunks)
-    attend(first)
+    for i in (3, 4, 5):
+        fetches[i].wait()
+
+    @pl.loop(0, CTX // 4)
+    def _(j):
+        attend(j)
+
+    other = at_z(1 - h)
+    arecv[0, pl.ds(p, 1)] = abuf[pl.ds(c, 1)]
+    arecv[1, pl.ds(p, 1)] = abuf[pl.ds(other, 1)]
+    for i in (8, 9, 10):
+        fetches[i].wait()
     pl.semaphore_wait(barrier, CTX - 1 + 2 * (E - 1))
+
+    send(w_all.at[h], w_all.at[h], ssem.at[7], early.at[0], other, e)
+
+    far_first = sorted(
+        ((i, j) for i in range(X) for j in range(Y)),
+        key=lambda d: -min(d[0], X - d[0]) - min(d[1], Y - d[1]),
+    )
+    for hh in (1, 0):
+        for i, j in far_first:
+            if i or j:
+                there = rem(x + i, X) * (2 * Y) + rem(y + j, Y)
+                block = there + rem(h + hh, 2) * Y
+                send(abuf.at[block], arecv.at[hh, p], ssem.at[0], a_sem.at[hh], there + h * Y, e)
 
     send(gg_all.at[h], gg_all.at[h], ssem.at[8], early.at[1], at_z(1 - h), e)
     spread = div(p, PB) == e
@@ -204,42 +252,47 @@
             res_recv[pl.ds(mine, 1), half] = res_ref[:, cols][None]
         g_recv[pl.ds(mine, 1)] = g_own[...][None]
 
-    send_chunk(first)
-
-    @pl.loop(1, n_chunks)
-    def _(i):
-        j = rem(first + i, n_chunks)
-        attend(j)
-        send_chunk(j)
-
-    send(wo_ref, w_all.at[h], ssem.at[7], early.at[0], at_z(1 - h), e)
-
-    arecv[pl.ds(c, 1)] = abuf[pl.ds(c, 1)]
-    wait_bytes(arecv.at[pl.ds(0, CTX - 1)], rsem.at[0])
-    levels = jnp.zeros((CTX, 128), F32)
-    for i in range(CTX):
-        line = jnp.sum(arecv[i, 32:40, :].astype(F32), axis=0, keepdims=True)
-        levels = jnp.where(iota((CTX, 128), 0) == i, line, levels)
-    weight = jnp.exp(levels - jnp.max(levels, axis=0, keepdims=True))
-    weight = weight / jnp.sum(weight, axis=0, keepdims=True)
-    weight = jnp.concatenate([weight, jnp.zeros((128 - CTX, 128), F32)], axis=0)
-    wt_s[...] = weight.T
-    columns = wt_s[pl.ds(pl.multiple_of(rem(c, 4) * 32, 32), 32), :]
-    attended = jnp.zeros((32, 128), F32)
-    for i in range(CTX):
-        attended = attended + arecv[i, 0:32, :].astype(F32) * columns[:, i : i + 1]
-    new = iota((32, 32), 0)
-    order = rem(new, 8) * 4 + div(new, 8)
-    swap = jnp.where(iota((32, 32), 1) == order, 1.0, 0.0).astype(BF16)
-    heads = dot(swap, attended.astype(BF16)).reshape(4, 1, 8, 128)
+    def combine(pairs, block):
+        levels = jnp.full((32, 128), -1e30, F32)
+        for i, (_, lines) in enumerate(pairs):
+            line = jnp.sum(lines(), axis=0, keepdims=True)
+            levels = jnp.where(iota((32, 128), 0) == i, line, levels)
+        top = jnp.max(levels, axis=0, keepdims=True)
+        weight = jnp.exp(levels - top)
+        total = jnp.sum(weight, axis=0, keepdims=True)
+        weight = jnp.concatenate([weight / total, jnp.zeros((96, 128), F32)], axis=0)
+        wt_s[...] = weight.T
+        columns = wt_s[pl.ds(pl.multiple_of(rem(block, 4) * 32, 32), 32), :]
+        attended = jnp.zeros((32, 128), F32)
+        for i, (rows, _) in enumerate(pairs):
+            attended = attended + rows() * columns[:, i : i + 1]
+        return attended, top + jnp.log(total)
+
+    def slab(ref, *at):
+        return (
+            lambda: ref[(*at, slice(0, 32))].astype(F32),
+            lambda: ref[(*at, slice(32, 40))].astype(F32),
+        )
+
+    wait_bytes(arecv.at[1, pl.ds(0, PL - 1)], a_sem.at[1])
+    attended, level = combine([slab(arecv, 1, i) for i in range(PL)], other)
+    a_out[0:32, :] = attended.astype(BF16)
+    a_out[32:40, :] = level_lines(level)
+    send(a_out, a_in, ssem.at[14], early.at[2 + 2 * PB], other, e)
+
+    wait_bytes(arecv.at[0, pl.ds(0, PL - 1)], a_sem.at[0])
+    own_part, own_level = combine([slab(arecv, 0, i) for i in range(PL)], c)
+    own_lines = jnp.where(row8 == 0, own_level, 0.0)
+    wait_bytes(a_in, early.at[2 + 2 * PB])
+    attended, _ = combine([(lambda: own_part, lambda: own_lines), slab(a_in)], c)
+    heads = dot(swap_s[...], attended.astype(BF16)).reshape(4, 1, 8, 128)
     att_all[:, pl.ds(p, 1)] = heads.astype(BF16)
-    for i in range(X):
-        for j in range(Y):
-            if i or j:
-                there = rem(x + i, X) * (2 * Y) + h * Y + rem(y + j, Y)
-                send(att_all.at[:, p], att_all.at[:, p], ssem.at[1], rsem.at[1], there, e)
-
-    wait_bytes(wo_ref, early.at[0])
+    for i, j in far_first:
+        if i or j:
+            there = rem(x + i, X) * (2 * Y) + h * Y + rem(y + j, Y)
+            send(att_all.at[:, p], att_all.at[:, p], ssem.at[1], rsem.at[1], there, e)
+
+    wait_bytes(w_all.at[h], early.at[0])
     wait_bytes(att_all.at[:, pl.ds(0, PL - 1)], rsem.at[1])
     rows = jnp.concatenate(
         [att_all[r].astype(F32).reshape(PL * 8, 128) for r in range(4)], axis=1
@@ -248,7 +301,7 @@
     rs_send[...] = partial.reshape(E, PB * 8, 256).astype(BF16)
     rs_recv[pl.ds(e, 1)] = rs_send[pl.ds(e, 1)]
 
-    for i in range(1, E):
+    for i in sorted(range(1, E), key=lambda i: abs(i - E // 2)):
         ee = rem(e + i, E)
         send(rs_send.at[ee], rs_recv.at[e], ssem.at[2], rsem.at[2], c, ee)
 
@@ -259,17 +312,8 @@
             wait_bytes(res_recv.at[i], early.at[2 + i])
             wait_bytes(g_recv.at[i], early.at[2 + PB + i])
 
-    pick_rows = E * PB * CAP
     table = g_recv[...].reshape(PB * 8, 128).astype(BF16)
-    pick = iota((pick_rows, 128), 0)
-    chooser = jnp.where(
-        iota((pick_rows, 128), 1) == div(pick, PB * CAP) * CAP + rem(pick, CAP), 1.0, 0.0
-    ).astype(BF16)
-    picks = dot_nt(chooser, table)
-    pick = iota((pick_rows, PB * 8), 0)
-    picks = jnp.where(
-        rem(div(pick, CAP), PB) == div(iota((pick_rows, PB * 8), 1), 8), picks, 0.0
-    ).astype(BF16)
+    picks = (dot_nt(picks_s[...], table) * mask_s[...]).astype(BF16)
     residual = jnp.concatenate(
         [
             jnp.concatenate([res_recv[i, half].astype(F32) for half in range(2)], axis=1)
@@ -285,7 +329,7 @@
     z_send[...] = dot(picks, stream.astype(BF16)).reshape(E, PB * CAP, 256).astype(BF16)
     xall[pl.ds(p, 1), pl.ds(hz, 1)] = z_send[pl.ds(e, 1)][None]
 
-    for i in range(1, 2 * E):
+    for i in sorted(range(1, 2 * E), key=lambda i: abs(i - E)):
         zz = rem(hz + i, 2 * E)
         ee = rem(zz, E)
         send(z_send.at[ee], xall.at[p, hz], ssem.at[3], rsem.at[3], at_z(div(zz, E)), ee)
@@ -326,29 +370,28 @@
         if i < Y:
             send(xall.at[p], xall.at[p], ssem.at[4], d_recv.at[i], ctx_of(0, i), e)
     expert_products(x, y)
-    for i in near_first(max(X, Y)):
-        if i < X:
-            xx, yy = source(i, 0)
-            src = xx * Y + yy
-            wait_bytes(xall.at[src], d_recv.at[i * Y])
-            for j in near_first(Y):
-                half = xall.at[src, low_half]
-                send(half, half, ssem.at[4], d_recv.at[i * Y + j], ctx_of(0, j), e)
-        if i < Y:
-            xx, yy = source(0, i)
-            src = xx * Y + yy
-            wait_bytes(xall.at[src], d_recv.at[i])
-            for j in near_first(X):
-                half = xall.at[src, high_half]
-                send(half, half, ssem.at[4], d_recv.at[PL + j * Y + i], ctx_of(j, 0), e)
-
-    @pl.loop(1, X)
-    def _(i):
-        expert_products(*source(i, 0))
-
-    @pl.loop(1, Y)
-    def _(i):
-        expert_products(*source(0, i))
+    def forward(i, j):
+        xx, yy = source(i, j)
+        src = xx * Y + yy
+        wait_bytes(xall.at[src], d_recv.at[i * Y + j])
+        if i:
+            half = xall.at[src, low_half]
+            for n in near_first(Y):
+                send(half, half, ssem.at[4], d_recv.at[i * Y + n], ctx_of(0, n), e)
+        else:
+            half = xall.at[src, high_half]
+            for n in near_first(X):
+                send(half, half, ssem.at[4], d_recv.at[PL + n * Y + j], ctx_of(n, 0), e)
+
+    def is_near(d):
+        return min(d[0], X - d[0]) + min(d[1], Y - d[1]) == 1
+
+    direct = [(i, 0) for i in range(1, X)] + [(0, j) for j in range(1, Y)]
+    for group in ([d for d in direct if is_near(d)], [d for d in direct if not is_near(d)]):
+        for i, j in group:
+            forward(i, j)
+        for i, j in group:
+            expert_products(*source(i, j))
 
     @pl.loop(0, (X - 1) * (Y - 1))
     def _(t):
@@ -362,9 +405,7 @@
     norm = lax.rsqrt(jnp.sum(sq_acc[...], axis=1, keepdims=True) / D + 1e-05)
     gate_val = accg[...] * norm
     act = ((gate_val / (1.0 + jnp.exp(-gate_val))) * (accu[...] * norm)).astype(BF16)
-    new = iota((S, S), 0)
-    order = rem(div(new, CAP), 2) * (PL * CAP) + div(new, 2 * CAP) * CAP + rem(new, CAP)
-    act = dot(jnp.where(iota((S, S), 1) == order, 1.0, 0.0).astype(BF16), act).astype(BF16)
+    act = dot(order_s[...], act).astype(BF16)
 
     weights[2].wait()
     for n in range(NCH):
@@ -430,9 +471,12 @@
 
     f_recv[pl.ds(hz, 1)] = f_send[pl.ds(hz, 1)]
     wait_bytes(f_recv.at[pl.ds(0, 2 * E - 1)], rsem.at[4])
-    out_ref[...] = jnp.sum(f_recv[...].astype(F32), axis=0).astype(BF16)
-
-    wait_bytes(abuf.at[pl.ds(0, CTX - 1)], ssem.at[0])
+    out_s[...] = jnp.sum(f_recv[...].astype(F32), axis=0).astype(BF16)
+    result = pltpu.make_async_copy(out_s, out_hbm, wsem.at[0])
+    result.start()
+
+    wait_bytes(abuf.at[pl.ds(0, 2 * (PL - 1))], ssem.at[0])
+    wait_bytes(a_out, ssem.at[14])
     wait_bytes(att_all.at[:, pl.ds(0, PL - 1)], ssem.at[1])
     wait_bytes(rs_send.at[pl.ds(0, E - 1)], ssem.at[2])
     wait_bytes(xall.at[0, pl.ds(0, 2 * E - 1)], ssem.at[3])
@@ -443,13 +487,14 @@
     wait_bytes(t_send.at[even, pl.ds(0, X - 1)], ssem.at[12])
     wait_bytes(t_send.at[odd, pl.ds(0, Y - 1)], ssem.at[13])
     wait_bytes(f_send.at[pl.ds(0, 2 * E - 1)], ssem.at[6])
-    wait_bytes(wo_ref, ssem.at[7])
+    wait_bytes(w_all.at[h], ssem.at[7])
     wait_bytes(gg_all.at[h], ssem.at[8])
 
     @pl.when(spread)
     def _():
         wait_bytes(f_recv.at[pl.ds(0, PL - 1), :, pl.ds(0, 256)], ssem.at[9])
         wait_bytes(f_recv.at[pl.ds(0, PL - 1), :, pl.ds(0, 256)], ssem.at[10])
+    result.wait()
 
 
 def local(queries, keys, values, out_proj, residual, gain, routes, gates, w_gate, w_up, w_down):
@@ -457,17 +502,30 @@
     CTX, PL, E = 2 * X * Y, X * Y, lax.axis_size("exp")
     PB, D, FF = PL // E, gain.shape[0], w_gate.shape[2]
     S, CE = 2 * PL * CAP, D // E
-    chunk_cols, side = 1024, max(X, Y)
+    chunk_cols, side = 512, max(X, Y)
     NCH = D // chunk_cols
-    vmem = pl.BlockSpec(memory_space=pltpu.VMEM)
     return pl.pallas_call(
         functools.partial(kernel, (X, Y, E, chunk_cols)),
         out_shape=jax.ShapeDtypeStruct((8, CE), BF16),
-        in_specs=[vmem] * 8 + [pl.BlockSpec(memory_space=pl.ANY)] * 3,
-        out_specs=vmem,
+        in_specs=[pl.BlockSpec(memory_space=pl.ANY)] * 11,
+        out_specs=pl.BlockSpec(memory_space=pl.ANY),
         scratch_shapes=[
+            pltpu.VMEM((8, CE), BF16),
+            pltpu.VMEM((CTX * 32, 128), BF16),
+            pltpu.VMEM((keys.shape[0], 128), BF16),
+            pltpu.VMEM((keys.shape[0], 128), BF16),
+            pltpu.VMEM((8, D), BF16),
+            pltpu.VMEM((CTX, 128), F32),
+            pltpu.VMEM((2, 8), jnp.int32),
+            pltpu.VMEM((2, 8), F32),
+            pltpu.VMEM((32, 32), BF16),
+            pltpu.VMEM((S, S), BF16),
+            pltpu.VMEM((E * PB * CAP, 128), BF16),
+            pltpu.VMEM((E * PB * CAP, PB * 8), F32),
             pltpu.VMEM((CTX, 40, 128), BF16),
-            pltpu.VMEM((CTX, 40, 128), BF16),
+            pltpu.VMEM((2, PL, 40, 128), BF16),
+            pltpu.VMEM((40, 128), BF16),
+            pltpu.VMEM((40, 128), BF16),
             pltpu.VMEM((128, 128), F32),
             pltpu.VMEM((4, PL, 8, 128), BF16),
             pltpu.VMEM((2, 512, 128), BF16),
@@ -493,10 +551,11 @@
             pltpu.VMEM((FF, D), BF16),
             pltpu.VMEM((FF, D), BF16),
             pltpu.VMEM((FF, D), BF16),
-            pltpu.SemaphoreType.DMA((3,)),
-            pltpu.SemaphoreType.DMA((14,)),
+            pltpu.SemaphoreType.DMA((11,)),
+            pltpu.SemaphoreType.DMA((15,)),
+            pltpu.SemaphoreType.DMA((2,)),
             pltpu.SemaphoreType.DMA((5,)),
-            pltpu.SemaphoreType.DMA((2 + 2 * PB,)),
+            pltpu.SemaphoreType.DMA((3 + 2 * PB,)),
             pltpu.SemaphoreType.DMA((2 * PL,)),
             pltpu.SemaphoreType.DMA((NCH,)),
             pltpu.SemaphoreType.DMA((NCH,)),

time: 72.4 us -> 67.3 us (0.930)
  Pallas kernels: 70.9 us -> 65.8 us
    pallas_call x1, Pallas kernels: 70.9 us -> 65.8 us  [local(): pl.pallas_call(functools.partial(kernel, (X, Y, E, chunk_cols)), out_shap...]
where the time goes in v3:
time: 67.3 us; the launch traced here: 67.1 us
  Pallas kernels  65.8 us (98%)
  local copies, waits for them, and re-layouts  1.3 us (2%)
    pallas_call x1, Pallas kernels, local(): pl.pallas_call(functools.partial(kernel, (X, Y, E, chunk_cols)), out_shap...  65.8 us

profile of v3, /device:TPU:1, one launch (start us, length us, event | category | flops | bytes accessed | tf_op | source)
XLA Modules:
  0.0 67.1 jit_solution(3881396948645219242)
XLA Ops:
  0.0 65.8 %shard_map.109 = bf16[8,512]{1,0:T(8,128)(2,1)} custom-call(bf16[1024,128]{1,0:T(8,128)(2,1)} %bitcast.16, bf16[1024,128]{1,0:T(8,128)(2,1)} %bitcast.17, bf16[1024,128]{1,0:T(8,128)(2,1)} %bitcast.18, bf16[512,128]{1,0:T(8,128)(2,1)} %wo_hbm.1, bf16[8,4096]{1,0:T(8,128)(2,1)} %res_hbm.1, f32[32,128]{1,0:T(8,128)} %bitcast.19, s32[2,8]{1,0:T(2,128)} %bitcast.20, ...), custom_call_target="tpu_custom_call" | custom-call | tf_op jit(solution)/shard_map/pallas_call | solution.py:507
  65.8 1.3 %copy.13 = bf16[8,512]{1,0:T(8,128)(2,1)} copy(bf16[8,512]{1,0:T(8,128)(2,1)} %shard_map.109) | data formatting | bytes 16384

commit v4 on v3

--- a/solution.py
+++ b/solution.py
@@ -56,7 +56,7 @@
     abuf, arecv, a_out, a_in, wt_s, att_all, w_all, rs_send, rs_recv, res_recv, g_own, g_recv, gg_all, f_sel,
     z_send, xall, sq_acc, accg, accu, sown, e_send, e_recv, t_send, t_recv, f_send, f_recv,
     wg_s, wu_s, wd_s,
-    wsem, ssem, a_sem, rsem, early, d_recv, e_sem, t_sem,
+    wsem, ssem, a_sem, z_sem, rsem, early, d_recv, e_sem, t_sem,
 ):
     X, Y, E, chunk_cols = geom
     PL, CTX = X * Y, 2 * X * Y
@@ -116,6 +116,86 @@
     for i in (6, 7, 3, 4, 5, 8, 9, 10, 0, 1, 2):
         fetches[i].start()
     weights = fetches[:3]
+
+    lane8 = iota((8, 128), 1)
+    row8 = iota((8, 128), 0)
+
+    scale = 1.0 / math.sqrt(128)
+    tail = key_rows - min(tokens, key_rows)
+
+    def level_lines(flat):
+        hi = flat.astype(BF16).astype(F32)
+        mid = (flat - hi).astype(BF16).astype(F32)
+        lo = flat - hi - mid
+        return jnp.where(
+            row8 == 0, hi, jnp.where(row8 == 1, mid, jnp.where(row8 == 2, lo, 0.0))
+        ).astype(BF16)
+
+    def attend(j):
+        q = q_ref[pl.ds(pl.multiple_of(j * 128, 128), 128), :]
+        s = dot_nt(q, k_ref[...]) * scale
+        token = j * 32 + parts(iota((128, key_rows - tail), 0), 4)[0]
+        limit = (CTX * key_rows - tokens) - c * key_rows + token
+        masked = jnp.where(
+            tail + iota((128, key_rows - tail), 1) <= limit, s[:, tail:], jnp.float32(-1e30)
+        )
+        s = jnp.concatenate([s[:, :tail], masked], axis=1) if tail else masked
+        m = jnp.max(s, axis=1, keepdims=True)
+        w = jnp.exp(s - m)
+        total = jnp.sum(w, axis=1, keepdims=True)
+        o = (dot(w.astype(BF16), v_ref[...]) / total).astype(BF16)
+        lse = m + jnp.log(total)
+        flat = jnp.sum(
+            jnp.where(iota((128, 128), 0) == iota((128, 128), 1), lse, 0.0), axis=0, keepdims=True
+        )
+        lines = level_lines(flat)
+        for r in range(4):
+            abuf[j * 4 + r, 0:32, :] = o[r * 32 : (r + 1) * 32, :]
+            abuf[j * 4 + r, 32:40, :] = lines
+
+    for i in (3, 4, 5):
+        fetches[i].wait()
+
+    other = at_z(1 - h)
+    far_first = sorted(
+        ((i, j) for i in range(X) for j in range(Y)),
+        key=lambda d: -min(d[0], X - d[0]) - min(d[1], Y - d[1]),
+    )
+
+    def attend_side(hh):
+        if Y % 4 == 0:
+            side = rem(h + hh, 2) * (Y // 4)
+
+            @pl.loop(0, PL // 4)
+            def _(i):
+                attend(div(i, Y // 4) * (Y // 2) + side + rem(i, Y // 4))
+
+        elif hh:
+
+            @pl.loop(0, CTX // 4)
+            def _(i):
+                attend(i)
+
+    def send_side(hh):
+        for i, j in far_first:
+            if i or j:
+                there = rem(x + i, X) * (2 * Y) + rem(y + j, Y)
+                block = there + rem(h + hh, 2) * Y
+                send(abuf.at[block], arecv.at[hh, p], ssem.at[0], a_sem.at[hh], there + h * Y, e)
+
+    attend_side(1)
+    fetches[10].wait()
+    pl.semaphore_wait(barrier, CTX - 1 + 2 * (E - 1))
+    send_side(1)
+
+    send(w_all.at[h], w_all.at[h], ssem.at[7], early.at[0], other, e)
+
+    attend_side(0)
+    send_side(0)
+    arecv[1, pl.ds(p, 1)] = abuf[pl.ds(other, 1)]
+    arecv[0, pl.ds(p, 1)] = abuf[pl.ds(c, 1)]
+    fetches[8].wait()
+    fetches[9].wait()
 
     new, old = iota((32, 32), 0), iota((32, 32), 1)
     head, token = parts(new, 8)
@@ -137,8 +217,6 @@
     fetches[6].wait()
     fetches[7].wait()
 
-    lane8 = iota((8, 128), 1)
-    row8 = iota((8, 128), 0)
     diagonal = iota((8, 8), 0) == iota((8, 8), 1)
     route = [
         jnp.sum(
@@ -170,66 +248,6 @@
         (high == h * PL + p) & (route[0] == e) & (slot[0] == s4), 1.0, 0.0
     ).astype(BF16)
 
-    scale = 1.0 / math.sqrt(128)
-    tail = key_rows - min(tokens, key_rows)
-
-    def level_lines(flat):
-        hi = flat.astype(BF16).astype(F32)
-        mid = (flat - hi).astype(BF16).astype(F32)
-        lo = flat - hi - mid
-        return jnp.where(
-            row8 == 0, hi, jnp.where(row8 == 1, mid, jnp.where(row8 == 2, lo, 0.0))
-        ).astype(BF16)
-
-    def attend(j):
-        q = q_ref[pl.ds(pl.multiple_of(j * 128, 128), 128), :]
-        s = dot_nt(q, k_ref[...]) * scale
-        token = j * 32 + parts(iota((128, key_rows - tail), 0), 4)[0]
-        limit = (CTX * key_rows - tokens) - c * key_rows + token
-        masked = jnp.where(
-            tail + iota((128, key_rows - tail), 1) <= limit, s[:, tail:], jnp.float32(-1e30)
-        )
-        s = jnp.concatenate([s[:, :tail], masked], axis=1) if tail else masked
-        m = jnp.max(s, axis=1, keepdims=True)
-        w = jnp.exp(s - m)
-        total = jnp.sum(w, axis=1, keepdims=True)
-        o = (dot(w.astype(BF16), v_ref[...]) / total).astype(BF16)
-        lse = m + jnp.log(total)
-        flat = jnp.sum(
-            jnp.where(iota((128, 128), 0) == iota((128, 128), 1), lse, 0.0), axis=0, keepdims=True
-        )
-        lines = level_lines(flat)
-        for r in range(4):
-            abuf[j * 4 + r, 0:32, :] = o[r * 32 : (r + 1) * 32, :]
-            abuf[j * 4 + r, 32:40, :] = lines
-
-    for i in (3, 4, 5):
-        fetches[i].wait()
-
-    @pl.loop(0, CTX // 4)
-    def _(j):
-        attend(j)
-
-    other = at_z(1 - h)
-    arecv[0, pl.ds(p, 1)] = abuf[pl.ds(c, 1)]
-    arecv[1, pl.ds(p, 1)] = abuf[pl.ds(other, 1)]
-    for i in (8, 9, 10):
-        fetches[i].wait()
-    pl.semaphore_wait(barrier, CTX - 1 + 2 * (E - 1))
-
-    send(w_all.at[h], w_all.at[h], ssem.at[7], early.at[0], other, e)
-
-    far_first = sorted(
-        ((i, j) for i in range(X) for j in range(Y)),
-        key=lambda d: -min(d[0], X - d[0]) - min(d[1], Y - d[1]),
-    )
-    for hh in (1, 0):
-        for i, j in far_first:
-            if i or j:
-                there = rem(x + i, X) * (2 * Y) + rem(y + j, Y)
-                block = there + rem(h + hh, 2) * Y
-                send(abuf.at[block], arecv.at[hh, p], ssem.at[0], a_sem.at[hh], there + h * Y, e)
-
     send(gg_all.at[h], gg_all.at[h], ssem.at[8], early.at[1], at_z(1 - h), e)
     spread = div(p, PB) == e
     mine = rem(p, PB)
@@ -332,14 +350,14 @@
     for i in sorted(range(1, 2 * E), key=lambda i: abs(i - E)):
         zz = rem(hz + i, 2 * E)
         ee = rem(zz, E)
-        send(z_send.at[ee], xall.at[p, hz], ssem.at[3], rsem.at[3], at_z(div(zz, E)), ee)
+        hh = div(zz, E)
+        send(z_send.at[ee], xall.at[p, hz], ssem.at[3], z_sem.at[rem(hh + h, 2)], at_z(hh), ee)
 
     sq_acc[...] = jnp.zeros_like(sq_acc)
     accg[...] = jnp.zeros_like(accg)
     accu[...] = jnp.zeros_like(accu)
     weights[0].wait()
     weights[1].wait()
-    wait_bytes(xall.at[p, pl.ds(0, 2 * E - 1)], rsem.at[3])
 
     def ctx_of(i, j):
         return rem(x + i, X) * (2 * Y) + h * Y + rem(y + j, Y)
@@ -347,7 +365,8 @@
     def source(i, j):
         return rem(x + X - i, X), rem(y + Y - j, Y)
 
-    low_half, high_half = pl.ds(0, E), pl.ds(E, E)
+    early_half = pl.ds(pl.multiple_of(h * E, E), E)
+    late_half = pl.ds(pl.multiple_of((1 - h) * E, E), E)
 
     def expert_products(xx, yy):
         src = xx * Y + yy
@@ -364,42 +383,51 @@
         sown[:, pl.ds(low, 128)] = own[:, :128]
         sown[:, pl.ds(high, 128)] = own[:, 128:]
 
-    for i in near_first(max(X, Y)):
-        if i < X:
-            send(xall.at[p], xall.at[p], ssem.at[4], d_recv.at[i * Y], ctx_of(i, 0), e)
-        if i < Y:
-            send(xall.at[p], xall.at[p], ssem.at[4], d_recv.at[i], ctx_of(0, i), e)
-    expert_products(x, y)
+    rows = sorted(((i, 0) for i in range(1, X)), key=lambda d: min(d[0], X - d[0]))
+    columns = sorted(((0, j) for j in range(1, Y)), key=lambda d: min(d[1], Y - d[1]))
+
+    def spread_half(half, first_sem):
+        for i, j in rows + columns:
+            block = xall.at[p, half]
+            send(block, block, ssem.at[4], d_recv.at[first_sem + i * Y + j], ctx_of(i, j), e)
+
     def forward(i, j):
         xx, yy = source(i, j)
-        src = xx * Y + yy
-        wait_bytes(xall.at[src], d_recv.at[i * Y + j])
-        if i:
-            half = xall.at[src, low_half]
-            for n in near_first(Y):
-                send(half, half, ssem.at[4], d_recv.at[i * Y + n], ctx_of(0, n), e)
-        else:
-            half = xall.at[src, high_half]
-            for n in near_first(X):
-                send(half, half, ssem.at[4], d_recv.at[PL + n * Y + j], ctx_of(n, 0), e)
-
-    def is_near(d):
-        return min(d[0], X - d[0]) + min(d[1], Y - d[1]) == 1
-
-    direct = [(i, 0) for i in range(1, X)] + [(0, j) for j in range(1, Y)]
-    for group in ([d for d in direct if is_near(d)], [d for d in direct if not is_near(d)]):
-        for i, j in group:
-            forward(i, j)
-        for i, j in group:
-            expert_products(*source(i, j))
+        half, first_sem = (early_half, 0) if i else (late_half, PL)
+        block = xall.at[xx * Y + yy, half]
+        wait_bytes(block, d_recv.at[first_sem + i * Y + j])
+        for n in near_first(Y) if i else near_first(X):
+            to = (0, n) if i else (n, 0)
+            first = i * Y + n if i else n * Y + j
+            send(block, block, ssem.at[4], d_recv.at[first_sem + first], ctx_of(*to), e)
+
+    def direct_products(i, j):
+        xx, yy = source(i, j)
+        half, first_sem = (late_half, PL) if i else (early_half, 0)
+        wait_bytes(xall.at[xx * Y + yy, half], d_recv.at[first_sem + i * Y + j])
+        expert_products(xx, yy)
+
+    wait_bytes(xall.at[p, pl.ds(0, E - 1)], z_sem.at[0])
+    spread_half(early_half, 0)
+    wait_bytes(xall.at[p, pl.ds(0, E)], z_sem.at[1])
+    spread_half(late_half, PL)
+    expert_products(x, y)
+    for d in rows + columns[:2]:
+        forward(*d)
+    for d in rows[:2]:
+        direct_products(*d)
+    for d in columns[2:]:
+        forward(*d)
+    for d in rows[2:] + columns:
+        direct_products(*d)
 
     @pl.loop(0, (X - 1) * (Y - 1))
     def _(t):
         i, j = div(t, Y - 1) + 1, rem(t, Y - 1) + 1
         xx, yy = source(i, j)
         src = xx * Y + yy
-        wait_bytes(xall.at[src, low_half], d_recv.at[i * Y + j])
-        wait_bytes(xall.at[src, high_half], d_recv.at[PL + i * Y + j])
+        wait_bytes(xall.at[src, early_half], d_recv.at[i * Y + j])
+        wait_bytes(xall.at[src, late_half], d_recv.at[PL + i * Y + j])
         expert_products(xx, yy)
 
     norm = lax.rsqrt(jnp.sum(sq_acc[...], axis=1, keepdims=True) / D + 1e-05)
@@ -554,6 +582,7 @@
             pltpu.SemaphoreType.DMA((11,)),
             pltpu.SemaphoreType.DMA((15,)),
             pltpu.SemaphoreType.DMA((2,)),
+            pltpu.SemaphoreType.DMA((2,)),
             pltpu.SemaphoreType.DMA((5,)),
             pltpu.SemaphoreType.DMA((3 + 2 * PB,)),
             pltpu.SemaphoreType.DMA((2 * PL,)),

time: 67.3 us -> 64.5 us (0.958)
  Pallas kernels: 65.8 us -> 63.1 us
    pallas_call x1, Pallas kernels: 65.8 us -> 63.1 us  [local(): pl.pallas_call(functools.partial(kernel, (X, Y, E, chunk_cols)), out_shap...]
where the time goes in v4:
time: 64.5 us; the launch traced here: 64.4 us
  Pallas kernels  63.1 us (98%)
  local copies, waits for them, and re-layouts  1.3 us (2%)
    pallas_call x1, Pallas kernels, local(): pl.pallas_call(functools.partial(kernel, (X, Y, E, chunk_cols)), out_shap...  63.1 us
    unnamed x1, local copies, waits for them, and re-layouts  1.3 us

profile of v4, /device:TPU:1, one launch (start us, length us, event | category | flops | bytes accessed | tf_op | source)
XLA Modules:
  0.0 64.4 jit_solution(12489393586204035671)
XLA Ops:
  0.0 63.1 %shard_map.109 = bf16[8,512]{1,0:T(8,128)(2,1)} custom-call(bf16[1024,128]{1,0:T(8,128)(2,1)} %bitcast.16, bf16[1024,128]{1,0:T(8,128)(2,1)} %bitcast.17, bf16[1024,128]{1,0:T(8,128)(2,1)} %bitcast.18, bf16[512,128]{1,0:T(8,128)(2,1)} %wo_hbm.1, bf16[8,4096]{1,0:T(8,128)(2,1)} %res_hbm.1, f32[32,128]{1,0:T(8,128)} %bitcast.19, s32[2,8]{1,0:T(2,128)} %bitcast.20, ...), custom_call_target="tpu_custom_call" | custom-call | tf_op jit(solution)/shard_map/pallas_call | solution.py:535
  63.1 1.3 %copy.13 = bf16[8,512]{1,0:T(8,128)(2,1)} copy(bf16[8,512]{1,0:T(8,128)(2,1)} %shard_map.109) | data formatting | bytes 16384

commit v5 on v4

--- a/solution.py
+++ b/solution.py
@@ -42,6 +42,10 @@
 
 def near_first(n):
     return sorted(range(1, n), key=lambda i: min(i, n - i))
+
+
+def far_peers(n):
+    return near_first(n)[::-1]
 
 
 def wait_bytes(ref, sem):
@@ -440,11 +444,11 @@
         down = dot(act, wd_s[:, n * chunk_cols : (n + 1) * chunk_cols])
         e_send[n] = down.reshape(X, Y, 2 * CAP, chunk_cols).astype(BF16)
         if n % 2 == 0:
-            for j in near_first(Y):
+            for j in far_peers(Y):
                 block = e_send.at[n, :, rem(y + j, Y)]
                 send(block, e_recv.at[n, j - 1, pl.ds(0, X)], ssem.at[5], e_sem.at[n], ctx_of(0, j), e)
         else:
-            for i in near_first(X):
+            for i in far_peers(X):
                 block = e_send.at[n, rem(x + i, X)]
                 send(block, e_recv.at[n, i - 1, pl.ds(0, Y)], ssem.at[11], e_sem.at[n], ctx_of(i, 0), e)
 
@@ -455,7 +459,7 @@
             for j in range(Y - 1):
                 line = line + e_recv[n, j, :X].astype(F32)
             t_send[n, :X] = line.astype(BF16)
-            for i in near_first(X):
+            for i in far_peers(X):
                 block = t_send.at[n, rem(x + i, X)]
                 send(block, t_recv.at[n, i - 1], ssem.at[12], t_sem.at[n], ctx_of(i, 0), e)
         else:
@@ -464,7 +468,7 @@
             for i in range(X - 1):
                 line = line + e_recv[n, i, :Y].astype(F32)
             t_send[n, :Y] = line.astype(BF16)
-            for j in near_first(Y):
+            for j in far_peers(Y):
                 block = t_send.at[n, rem(y + j, Y)]
                 send(block, t_recv.at[n, j - 1], ssem.at[13], t_sem.at[n], ctx_of(0, j), e)
 

time: 64.5 us -> 64.1 us (level)
  no operation moved by 1% of the time
where the time goes in v5:
time: 64.1 us; the launch traced here: 64 us
  Pallas kernels  62.7 us (98%)
  local copies, waits for them, and re-layouts  1.3 us (2%)
    pallas_call x1, Pallas kernels, local(): pl.pallas_call(functools.partial(kernel, (X, Y, E, chunk_cols)), out_shap...  62.7 us
    unnamed x1, local copies, waits for them, and re-layouts  1.3 us

profile of v5, /device:TPU:1, one launch (start us, length us, event | category | flops | bytes accessed | tf_op | source)
XLA Modules:
  0.0 64.0 jit_solution(15776441146026804843)
XLA Ops:
  0.0 62.7 %shard_map.109 = bf16[8,512]{1,0:T(8,128)(2,1)} custom-call(bf16[1024,128]{1,0:T(8,128)(2,1)} %bitcast.16, bf16[1024,128]{1,0:T(8,128)(2,1)} %bitcast.17, bf16[1024,128]{1,0:T(8,128)(2,1)} %bitcast.18, bf16[512,128]{1,0:T(8,128)(2,1)} %wo_hbm.1, bf16[8,4096]{1,0:T(8,128)(2,1)} %res_hbm.1, f32[32,128]{1,0:T(8,128)} %bitcast.19, s32[2,8]{1,0:T(2,128)} %bitcast.20, ...), custom_call_target="tpu_custom_call" | custom-call | tf_op jit(solution)/shard_map/pallas_call | solution.py:539
  62.7 1.3 %copy.13 = bf16[8,512]{1,0:T(8,128)(2,1)} copy(bf16[8,512]{1,0:T(8,128)(2,1)} %shard_map.109) | data formatting | bytes 16384
